TPU v7x, 128 devices: a whole 4x4x4 slice. The times are simulated.
128 devices in a mesh: gx: 8 (over x, core), gy: 16 (over z, y).
Axes of the slice: x: 4, y: 4, z: 4, core: 2. Of those that a mesh axis runs over, the one named last changes fastest.
Arguments:
- forcing: float32 [2048, 8192], P('gx', 'gy'), may hold values from -8 to 8
- bathymetry: float32 [2048, 8192], P('gx', 'gy'), may hold values from 0.1 to 10
- ocean_mask: int32 [2048, 8192], P('gx', 'gy'), may hold values 0 or 1
- aggregate_id: int32 [32, 128], P('gx', 'gy'), may hold values from 0 to 511, as said below
- coarse_inverse: float32 [512, 512], P(('gx', 'gy')), may hold values from -1 to 1
Outputs:
- solution: float32 [2048, 8192], P('gx', 'gy')
- residual: float32 [2048, 8192], P('gx', 'gy')
Inputs may be any that keep to these rules, and one draw needn't show every extreme that they name: `aggregate_id`: each aggregate holds exactly 8 tiles, consecutive in the row-major order of tiles.
All inputs are finite; a program needn't handle non-finite values. No bound on the sum of `ocean_mask` on one device may be relied on, other than what follows from the above.
Results may differ from a plain program's by a relative error of at most 0.00075.
Values sent between devices are 32-bit elements; how exact they have to be, the bound alone decides.
A program may use at most 128 MiB of HBM per device.

v0:
```python
import jax
import jax.numpy as jnp
from jax import lax
from jax.sharding import PartitionSpec as P

TILE = 64
NAGG = 512
KB = 8
CYCLES = 2


highest = lax.Precision.HIGHEST
SHIFT_REL = 0.001


def padded_2(cells, sides, width):
    for axis, dim in sides:
        count = lax.axis_size(axis)
        ends = count - 1
        head = lax.slice_in_dim(cells, 0, width, axis=dim)
        tail = lax.slice_in_dim(cells, cells.shape[dim] - width, cells.shape[dim], axis=dim)
        cells = jnp.concatenate(
            [
                lax.ppermute(tail, axis, [(i, (i + 1) % count) for i in range(ends)]),
                cells,
                lax.ppermute(head, axis, [((i + 1) % count, i) for i in range(ends)]),
            ],
            axis=dim,
        )
    return cells


def face_coefficients(wet_padded):
    row_faces = jnp.minimum(wet_padded[1:, :], wet_padded[:-1, :])
    col_faces = jnp.minimum(wet_padded[:, 1:], wet_padded[:, :-1])
    return (row_faces, col_faces)


def operate(padded, row_faces, col_faces):
    row_flux = row_faces * (padded[1:, :] - padded[:-1, :])
    col_flux = col_faces * (padded[:, 1:] - padded[:, :-1])
    centre = padded[1:-1, 1:-1]
    return (
        centre - row_flux[1:, 1:-1] + row_flux[:-1, 1:-1] - col_flux[1:-1, 1:] + col_flux[1:-1, :-1]
    )


def crop_faces(row_faces, col_faces):
    return (row_faces, col_faces)


def change_matrix(spectral_shift):
    row_ids = jnp.arange(KB + 1)[:, None]
    col_ids = jnp.arange(KB)[None, :]
    below = jnp.where(col_ids == 0, 1.0, 0.5)
    values = jnp.where(
        row_ids == col_ids,
        1.0,
        jnp.where(row_ids == col_ids + 1, below, jnp.where(row_ids == col_ids - 1, 0.5, 0.0)),
    )
    return spectral_shift * values.astype(jnp.float32)


def lower_factor(matrix):
    order = matrix.shape[0]
    row_ids = jnp.arange(order)
    factor = jnp.zeros_like(matrix)
    for column in range(order):
        reduced = matrix[:, column] - jnp.sum(
            factor[:, :column] * factor[column, :column][None, :], axis=1
        )
        pivot = jnp.sqrt(reduced[column])
        entries = jnp.where(row_ids >= column, reduced / pivot, 0.0)
        factor = factor.at[:, column].set(entries)
    return factor


def upper_solve(triangle, right):
    order = triangle.shape[0]
    solved = jnp.zeros_like(right)
    for row in range(order - 1, -1, -1):
        rest = jnp.sum(triangle[row, row + 1 :] * solved[row + 1 :])
        solved = solved.at[row].set((right[row] - rest) / triangle[row, row])
    return solved


def small_solve(gram, spectral_shift):
    shifted = gram + SHIFT_REL * jnp.diag(jnp.diagonal(gram))
    chol_lower = lower_factor(shifted)
    chol_upper = chol_lower.T
    change = change_matrix(spectral_shift)
    projected = jnp.dot(chol_upper, change, precision=highest)
    target = chol_upper[:, 0]
    ortho_list = []
    triangle = jnp.zeros((KB, KB), jnp.float32)
    for column in range(KB):
        vector = projected[:, column]
        for passes in range(2):
            if column > 0:
                earlier_cols = jnp.stack(ortho_list, axis=1)
                amounts = jnp.dot(earlier_cols.T, vector, precision=highest)
                triangle = triangle.at[:column, column].add(amounts)
                vector = vector - jnp.dot(earlier_cols, amounts, precision=highest)
        length = jnp.sqrt(jnp.sum(vector * vector))
        triangle = triangle.at[column, column].set(length)
        ortho_list.append(vector / length)
    ortho_cols = jnp.stack(ortho_list, axis=1)
    small_rhs = jnp.dot(ortho_cols.T, target, precision=highest)
    weights = upper_solve(triangle, small_rhs)
    combined = jnp.dot(change, weights, precision=highest)
    return (weights, combined)


def plain_step(earlier, current, row_part, col_part, spectral_shift):
    padded = padded_2(current, (("gx", 0), ("gy", 1)), 1)
    applied = operate(padded, row_part, col_part) / spectral_shift - current
    if earlier is None:
        return applied
    return 2.0 * applied - earlier


def on_device(forcing, bathymetry, ocean_mask, aggregate_id, coarse_inverse):
    height, breadth = forcing.shape
    tile_rows = height // TILE
    tile_cols = breadth // TILE
    ocean = ocean_mask.astype(jnp.float32)
    wet_depth = bathymetry * ocean
    halo_depth = 1
    wet_padded = padded_2(wet_depth, (("gx", 0), ("gy", 1)), halo_depth)
    row_faces, col_faces = face_coefficients(wet_padded)
    diagonal = (
        1.0
        + row_faces[halo_depth : halo_depth + height, halo_depth : halo_depth + breadth]
        + row_faces[halo_depth - 1 : halo_depth + height - 1, halo_depth : halo_depth + breadth]
        + col_faces[halo_depth : halo_depth + height, halo_depth : halo_depth + breadth]
        + col_faces[halo_depth : halo_depth + height, halo_depth - 1 : halo_depth + breadth - 1]
    )
    spectral_shift = lax.pmax(jnp.max(diagonal), ("gx", "gy"))
    row_one, col_one = crop_faces(row_faces, col_faces)
    tile_index = aggregate_id.reshape(-1)
    onehot = (tile_index[:, None] == jnp.arange(NAGG, dtype=jnp.int32)[None, :]).astype(jnp.float32)
    colmap = (
        jnp.arange(breadth, dtype=jnp.int32)[:, None] // TILE
        == jnp.arange(tile_cols, dtype=jnp.int32)[None, :]
    ).astype(jnp.float32)
    rowmap = (
        jnp.arange(height, dtype=jnp.int32)[:, None] // TILE
        == jnp.arange(tile_rows, dtype=jnp.int32)[None, :]
    ).astype(jnp.float32)
    solution = jnp.zeros_like(forcing)
    residual = forcing * ocean
    for cycle in range(CYCLES):
        fields = residual[None]
        members = fields.shape[0]
        row_sums = (fields * ocean[None]).reshape(members, tile_rows, TILE, breadth).sum(axis=2)
        tile_sums = jnp.einsum("nrc,ct->nrt", row_sums, colmap, precision=highest)
        coarse_rhs = lax.psum(
            jnp.dot(tile_sums.reshape(members, tile_rows * tile_cols), onehot, precision=highest)[
                0
            ],
            ("gx", "gy"),
        )
        whole_inverse = lax.all_gather(coarse_inverse, ("gx", "gy"), axis=0, tiled=True)
        coarse_values = jnp.dot(whole_inverse, coarse_rhs, precision=highest)
        tile_values = jnp.dot(onehot, coarse_values, precision=highest).reshape(
            tile_rows, tile_cols
        )
        spread = jnp.dot(
            jnp.dot(rowmap, tile_values, precision=highest), colmap.T, precision=highest
        )
        correction = spread * ocean
        solution = solution + correction
        correction_pad = padded_2(correction, (("gx", 0), ("gy", 1)), 1)
        residual = residual - operate(correction_pad, row_one, col_one)
        krylov = [residual]
        for index in range(KB):
            earlier = None if index == 0 else krylov[-2]
            krylov.append(plain_step(earlier, krylov[-1], row_one, col_one, spectral_shift))
        fields = jnp.stack(krylov)
        stacked = fields.reshape(KB + 1, height * breadth)
        gram_local = jnp.einsum("ai,bi->ab", stacked, stacked, precision=highest)
        gram = lax.psum(gram_local, ("gx", "gy"))
        weights, combined = small_solve(gram, spectral_shift)
        solution = solution + jnp.dot(weights, stacked[:KB], precision=highest).reshape(
            height, breadth
        )
        residual = residual - jnp.dot(combined, stacked, precision=highest).reshape(height, breadth)
    return (solution, residual)


def solution(mesh):
    return jax.shard_map(
        on_device,
        mesh=mesh,
        in_specs=(
            P("gx", "gy"),
            P("gx", "gy"),
            P("gx", "gy"),
            P("gx", "gy"),
            P(("gx", "gy"), None),
        ),
        out_specs=(P("gx", "gy"), P("gx", "gy")),
        check_vma=False,
    )
```

profile of v0, /device:TPU:1, one launch (start us, length us, event | category | flops | bytes accessed | tf_op | source)
XLA Modules:
  0.0 1137.4 jit_solution(18115529422173461289)
XLA Ops:
  9.2 4.5 collective-permute-start
  18.3 67.2 %psum.28 = f32[512]{0:T(512)S(1)} all-reduce(f32[512]{0:T(512)S(1)} %bitcast.924), channel_id=1, replica_groups=mesh['gx'=8,'gy'=16] {'gx','gy'}, use_global_device_ids=true, to_apply=%region_1.0 | all-reduce | flops 512 | bytes 4096 | tf_op jit(solution)/shard_map/psum | solution.py:157
  116.1 4.7 collective-permute-start.8
  126.4 5.1 collective-permute-start.10
  132.8 66.0 %pmax.7 = f32[]{:T(128)} all-reduce(f32[]{:T(128)} %fusion.133), channel_id=1, replica_groups=mesh['gx'=8,'gy'=16] {'gx','gy'}, use_global_device_ids=true, to_apply=%region_4.5 | all-reduce | flops 1 | bytes 8 | tf_op jit(solution)/shard_map/pmax | solution.py:138
  220.3 4.4 collective-permute-start.16
  234.6 4.1 collective-permute-done.19
  240.5 4.4 collective-permute-start.20
  250.0 4.5 collective-permute-start.22
  256.5 4.1 collective-permute-done.23
  277.6 4.1 collective-permute-done.27
  297.8 4.1 collective-permute-done.31
  353.3 26.6 %fusion.8 = f32[9,9]{1,0:T(8,128)S(1)} fusion(f32[9,256,512]{2,1,0:T(8,128)S(1)} %get-tuple-element.978), kind=kOutput, calls=%fused_computation.14 | convolution fusion | flops 127401984 | bytes 4718916 | tf_op jit(solution)/shard_map/ai,bi->ab/dot_general | solution.py:181
  379.9 66.9 %psum.29 = f32[9,9]{1,0:T(8,128)S(1)} all-reduce(f32[9,9]{1,0:T(8,128)S(1)} %fusion.8), channel_id=1, replica_groups=mesh['gx'=8,'gy'=16] {'gx','gy'}, use_global_device_ids=true, to_apply=%region_5.6 | all-reduce | flops 81 | bytes 648 | tf_op jit(solution)/shard_map/psum | solution.py:182
  565.1 21.1 %stack.348 = f32[9,131072]{1,0:T(8,128)} concatenate(f32[1,131072]{1,0:T(1,128)} %bitcast.869, f32[1,131072]{1,0:T(1,128)} %bitcast.871, f32[1,131072]{1,0:T(1,128)} %bitcast.873, f32[1,131072]{1,0:T(1,128)} %bitcast.875, f32[1,131072]{1,0:T(1,128)} %bitcast.877, f32[1,131072]{1,0:T(1,128)} %bitcast.879, f32[1,131072]{1,0:T(1,128)} %bitcast.881, f32[1,131072]{1,0:T(1,128)} %bitcast.883, ...), dimensions={0} | concatenate | bytes 9437184 | tf_op jit(solution)/shard_map/stack | solution.py:179
  586.2 8.2 copy.84
  595.0 8.3 fusion.2
  604.8 62.6 %psum.30 = f32[512]{0:T(512)S(1)} all-reduce(f32[512]{0:T(512)S(1)} %bitcast.925), channel_id=1, replica_groups=mesh['gx'=8,'gy'=16] {'gx','gy'}, use_global_device_ids=true, to_apply=%region_42.43 | all-reduce | flops 512 | bytes 4096 | tf_op jit(solution)/shard_map/psum | solution.py:157
  721.1 4.4 collective-permute-done.51
  727.4 4.2 collective-permute-start.52
  747.8 4.4 collective-permute-start.56
  817.2 4.6 collective-permute-start.70
  823.1 12.1 %stack.172 = f32[8,131072]{1,0:T(8,128)} concatenate(f32[1,131072]{1,0:T(1,128)} %bitcast.870, f32[1,131072]{1,0:T(1,128)} %bitcast.872, f32[1,131072]{1,0:T(1,128)} %bitcast.874, f32[1,131072]{1,0:T(1,128)} %bitcast.876, f32[1,131072]{1,0:T(1,128)} %bitcast.878, f32[1,131072]{1,0:T(1,128)} %bitcast.880, f32[1,131072]{1,0:T(1,128)} %bitcast.882, f32[1,131072]{1,0:T(1,128)} %bitcast.884), dimensions={0} | concatenate | bytes 8388608 | tf_op jit(solution)/shard_map/stack | solution.py:179
  844.8 4.4 fusion.244
  852.7 4.8 collective-permute-start.74
  866.3 11.8 %stack.381 = f32[8,131072]{1,0:T(8,128)} concatenate(f32[1,131072]{1,0:T(1,128)S(1)} %bitcast.885, f32[1,131072]{1,0:T(1,128)} %bitcast.887, f32[1,131072]{1,0:T(1,128)} %bitcast.889, f32[1,131072]{1,0:T(1,128)} %bitcast.891, f32[1,131072]{1,0:T(1,128)S(1)} %bitcast.893, f32[1,131072]{1,0:T(1,128)} %bitcast.895, f32[1,131072]{1,0:T(1,128)} %bitcast.897, f32[1,131072]{1,0:T(1,128)} %bitcast.899), dimensions={0} | concatenate | bytes 8388608 | tf_op jit(solution)/shard_map/stack | solution.py:179
  882.9 17.0 %fusion.11 = f32[9,9]{1,0:T(8,128)S(1)} fusion(f32[9,256,512]{2,1,0:T(8,128)} %get-tuple-element.956), kind=kOutput, calls=%fused_computation.15 | convolution fusion | flops 127401984 | bytes 4718916 | tf_op jit(solution)/shard_map/ai,bi->ab/dot_general | solution.py:181
  899.9 68.9 %psum.31 = f32[9,9]{1,0:T(8,128)S(1)} all-reduce(f32[9,9]{1,0:T(8,128)S(1)} %fusion.11), channel_id=1, replica_groups=mesh['gx'=8,'gy'=16] {'gx','gy'}, use_global_device_ids=true, to_apply=%region_43.44 | all-reduce | flops 81 | bytes 648 | tf_op jit(solution)/shard_map/psum | solution.py:182
  1084.5 6.7 fusion.232
  1091.2 20.3 %stack.383 = f32[9,131072]{1,0:T(8,128)} concatenate(f32[1,131072]{1,0:T(1,128)S(1)} %bitcast.886, f32[1,131072]{1,0:T(1,128)S(1)} %bitcast.888, f32[1,131072]{1,0:T(1,128)S(1)} %bitcast.890, f32[1,131072]{1,0:T(1,128)S(1)} %bitcast.892, f32[1,131072]{1,0:T(1,128)S(1)} %bitcast.894, f32[1,131072]{1,0:T(1,128)} %bitcast.896, f32[1,131072]{1,0:T(1,128)} %bitcast.898, ...), dimensions={0} | concatenate | bytes 9437184 | tf_op jit(solution)/shard_map/stack | solution.py:179
  1111.6 8.2 copy.94
  1120.3 8.1 fusion
  (674 shorter events, 508.6 us)
Async XLA Ops:
  7.2 83.1 %all-gather.3.cloned.1.call-start = ((), (), s32[]{:S(2)}) async-start(), calls=%async_computation | async-start | bytes 1056768 | tf_op jit(solution)/shard_map/all_gather | solution.py:163
  9.2 90.1 %collective-permute-start = (f32[1,512]{1,0:T(1,128)S(1)}, f32[1,512]{1,0:T(1,128)S(1)}, u32[]{:S(2)}, u32[]{:S(2)}) collective-permute-start(f32[1,512]{1,0:T(1,128)S(1)} %get-tuple-element.1072), channel_id=1, source_target_pairs={{0,16},{16,32},{32,48},{48,64},{64,80},{80,96},{96,112},{1,17},{17... | collective-permute-start | bytes 6152 | tf_op jit(solution)/shard_map/ppermute | solution.py:24
  13.7 85.6 %collective-permute-start.1 = (f32[1,512]{1,0:T(1,128)S(1)}, f32[1,512]{1,0:T(1,128)S(1)}, u32[]{:S(2)}, u32[]{:S(2)}) collective-permute-start(f32[1,512]{1,0:T(1,128)S(1)} %get-tuple-element.1073), channel_id=1, source_target_pairs={{16,0},{32,16},{48,32},{64,48},{80,64},{96,80},{112,96},{17,1},{33... | collective-permute-start | bytes 6152 | tf_op jit(solution)/shard_map/ppermute | solution.py:26
  94.0 10.8 collective-permute-start.4
  97.3 7.4 collective-permute-start.5
  99.4 8.9 collective-permute-start.3
  100.7 7.6 collective-permute-start.2
  106.9 6.8 collective-permute-start.7
  116.1 7.7 collective-permute-start.8
  126.4 72.4 %collective-permute-start.10 = (f32[258,1]{1,0:T(8,128)}, f32[258,1]{1,0:T(8,128)}, u32[]{:S(2)}, u32[]{:S(2)}) collective-permute-start(f32[258,1]{1,0:T(8,128)} %get-tuple-element.1032), channel_id=1, source_target_pairs={{0,1},{1,2},{2,3},{3,4},{4,5},{5,6},{6,7},{7,8},{8,9},{9,10},{10,1... | collective-permute-start | bytes 3104 | tf_op jit(solution)/shard_map/ppermute | solution.py:24
  131.5 67.3 %collective-permute-start.11 = (f32[258,1]{1,0:T(8,128)}, f32[258,1]{1,0:T(8,128)}, u32[]{:S(2)}, u32[]{:S(2)}) collective-permute-start(f32[258,1]{1,0:T(8,128)} %get-tuple-element.1033), channel_id=1, source_target_pairs={{1,0},{2,1},{3,2},{4,3},{5,4},{6,5},{7,6},{8,7},{9,8},{10,9},{11,1... | collective-permute-start | bytes 3104 | tf_op jit(solution)/shard_map/ppermute | solution.py:26
  220.3 7.0 collective-permute-start.16
  232.6 6.1 collective-permute-start.19
  240.5 7.0 collective-permute-start.20
  250.0 6.5 collective-permute-start.22
  262.4 6.7 collective-permute-start.24
  315.6 6.1 collective-permute-start.35
  323.5 9.1 collective-permute-start.36
  332.7 18.0 %collective-permute-start.38 = (f32[258,1]{1,0:T(8,128)S(1)}, f32[258,1]{1,0:T(8,128)S(1)}, u32[]{:S(2)}, u32[]{:S(2)}) collective-permute-start(f32[258,1]{1,0:T(8,128)S(1)} %get-tuple-element.1018), channel_id=1, source_target_pairs={{0,1},{1,2},{2,3},{3,4},{4,5},{5,6},{6,7},{7,8},{8,9},{9,10},{10,1... | collective-permute-start | bytes 3104 | tf_op jit(solution)/shard_map/ppermute | solution.py:24
  336.4 14.3 %collective-permute-start.39 = (f32[258,1]{1,0:T(8,128)S(1)}, f32[258,1]{1,0:T(8,128)S(1)}, u32[]{:S(2)}, u32[]{:S(2)}) collective-permute-start(f32[258,1]{1,0:T(8,128)S(1)} %get-tuple-element.1019), channel_id=1, source_target_pairs={{1,0},{2,1},{3,2},{4,3},{5,4},{6,5},{7,6},{8,7},{9,8},{10,9},{11,1... | collective-permute-start | bytes 3104 | tf_op jit(solution)/shard_map/ppermute | solution.py:26
  679.4 6.2 collective-permute-start.43
  699.1 6.1 collective-permute-start.47
  719.1 6.4 collective-permute-start.51
  727.4 6.1 collective-permute-start.52
  739.9 6.1 collective-permute-start.55
  747.8 6.3 collective-permute-start.56
  817.2 18.0 %collective-permute-start.70 = (f32[258,1]{1,0:T(8,128)}, f32[258,1]{1,0:T(8,128)}, u32[]{:S(2)}, u32[]{:S(2)}) collective-permute-start(f32[258,1]{1,0:T(8,128)} %get-tuple-element.1002), channel_id=1, source_target_pairs={{0,1},{1,2},{2,3},{3,4},{4,5},{5,6},{6,7},{7,8},{8,9},{9,10},{10,1... | collective-permute-start | bytes 3104 | tf_op jit(solution)/shard_map/ppermute | solution.py:24
  821.8 13.4 %collective-permute-start.71 = (f32[258,1]{1,0:T(8,128)}, f32[258,1]{1,0:T(8,128)}, u32[]{:S(2)}, u32[]{:S(2)}) collective-permute-start(f32[258,1]{1,0:T(8,128)} %get-tuple-element.1003), channel_id=1, source_target_pairs={{1,0},{2,1},{3,2},{4,3},{5,4},{6,5},{7,6},{8,7},{9,8},{10,9},{11,1... | collective-permute-start | bytes 3104 | tf_op jit(solution)/shard_map/ppermute | solution.py:26
  840.5 11.5 %collective-permute-start.72 = (f32[1,512]{1,0:T(1,128)S(1)}, f32[1,512]{1,0:T(1,128)S(1)}, u32[]{:S(2)}, u32[]{:S(2)}) collective-permute-start(f32[1,512]{1,0:T(1,128)S(1)} %get-tuple-element.1038), channel_id=1, source_target_pairs={{0,16},{16,32},{32,48},{48,64},{64,80},{80,96},{96,112},{1,17},{17... | collective-permute-start | bytes 6152 | tf_op jit(solution)/shard_map/ppermute | solution.py:24
  842.7 9.2 collective-permute-start.73
  852.7 25.4 %collective-permute-start.74 = (f32[258,1]{1,0:T(8,128)}, f32[258,1]{1,0:T(8,128)}, u32[]{:S(2)}, u32[]{:S(2)}) collective-permute-start(f32[258,1]{1,0:T(8,128)} %get-tuple-element.1000), channel_id=1, source_target_pairs={{0,1},{1,2},{2,3},{3,4},{4,5},{5,6},{6,7},{7,8},{8,9},{9,10},{10,1... | collective-permute-start | bytes 3104 | tf_op jit(solution)/shard_map/ppermute | solution.py:24
  857.5 20.6 %collective-permute-start.75 = (f32[258,1]{1,0:T(8,128)}, f32[258,1]{1,0:T(8,128)}, u32[]{:S(2)}, u32[]{:S(2)}) collective-permute-start(f32[258,1]{1,0:T(8,128)} %get-tuple-element.1001), channel_id=1, source_target_pairs={{1,0},{2,1},{3,2},{4,3},{5,4},{6,5},{7,6},{8,7},{9,8},{10,9},{11,1... | collective-permute-start | bytes 3104 | tf_op jit(solution)/shard_map/ppermute | solution.py:26
  (73 other events, 1403.5 us)
Sparse Core Ops, SparseCore 0:
  10.8 67.1 all-gather.2
where the time goes:
time: 1160 us; the launch traced here: 1140 us
  blocking collectives  332 us (29%)
  starting transfers between devices  199 us (17%)
  local copies, waits for them, and re-layouts  188 us (16%)
  matrix products  138 us (12%)
  waiting for transfers between devices  107 us (9%)
  other arithmetic  95.1 us (8%)
  between operations  77.9 us (7%)
    ppermute x38, starting transfers between devices, padded_2(): lax.ppermute(tail, axis, [(i, (i + 1) % count) for i in range(ends)])  137 us
    psum x2, blocking collectives, on_device(): gram = lax.psum(gram_local, ('gx', 'gy'))  136 us
    psum x2, blocking collectives, on_device(): lax.psum(jnp.dot(tile_sums.reshape(members, tile_rows * tile_cols), oneho...  130 us
    ppermute x38, waiting for transfers between devices, padded_2(): lax.ppermute(head, axis, [((i + 1) % count, i) for i in range(ends)])  96.8 us
    pmax x1, blocking collectives, on_device(): spectral_shift = lax.pmax(jnp.max(diagonal), ('gx', 'gy'))  66 us
    another operation x4, local copies, waits for them, and re-layouts, on_device(): fields = jnp.stack(krylov)  65.3 us
    ppermute x38, starting transfers between devices, padded_2(): lax.ppermute(head, axis, [((i + 1) % count, i) for i in range(ends)])  62.3 us
    dot_general x24, matrix products, small_solve(): amounts = jnp.dot(earlier_cols.T, vector, precision=highest)  47.3 us
  transfers between devices with their start and end apart: 77, of which 43 were waited for; matrix products, arithmetic and copies ran while one was open for 6% of the time, Pallas kernels for 0%

commit v1 on v0

v1 whole, which is shorter than its diff:
```python
import functools

import jax
import jax.numpy as jnp
from jax import lax
from jax.experimental import pallas as pl
from jax.experimental.pallas import tpu as pltpu
from jax.sharding import PartitionSpec as P

TILE = 64
KB = 8
CYCLES = 2
SHIFT_REL = 0.001
DEPTH = KB * CYCLES
LANES = 128
PAD = 8
OWN = PAD + DEPTH
ROW_STEP = 16
GROUPS = 4
MESH = pl.DeviceIdType.MESH
highest = lax.Precision.HIGHEST
SIDES = ((-1, 0), (1, 0), (0, -1), (0, 1), (-1, -1), (-1, 1), (1, -1), (1, 1))
NORTH, SOUTH, WEST, EAST, NW, NE, SW, SE = range(8)


def sub_total(x):
    for shift in (4, 2, 1):
        x = x + pltpu.roll(x, shift, 0)
    return x


def splat_sum(x):
    return jnp.broadcast_to(jnp.sum(sub_total(x), axis=1, keepdims=True), x.shape)


def fold(x):
    total = x[0:8]
    for start in range(8, x.shape[0], 8):
        total = total + x[start : start + 8]
    return total


def tall(x, rows):
    return jnp.concatenate([x] * (rows // 8), axis=0)


def small_solve(vv, vp):
    n = KB + 1
    moment = [None] * (2 * KB + 1)
    moment[0], moment[1] = vv[0], vp[1]
    for k in range(1, n):
        moment[2 * k] = 2.0 * vv[k] - vv[0]
    for k in range(2, n):
        moment[2 * k - 1] = 2.0 * vp[k] - vp[1]
    upper = [[None] * n for _ in range(n)]
    for j in range(n):
        reduced = vv[j] * (1.0 + SHIFT_REL)
        for k in range(j):
            reduced = reduced - upper[k][j] * upper[k][j]
        root = jnp.sqrt(reduced)
        upper[j][j] = root
        inverse = 1.0 / root
        for i in range(j + 1, n):
            if i - j == 1:
                entry = vp[i]
            else:
                entry = 0.5 * (moment[i + j] + moment[i - j])
            for k in range(j):
                entry = entry - upper[k][j] * upper[k][i]
            upper[j][i] = entry * inverse
    hess = [[None] * KB for _ in range(n)]
    for j in range(KB):
        below = 1.0 if j == 0 else 0.5
        for i in range(j + 2):
            entry = below * upper[i][j + 1]
            if i <= j:
                entry = entry + upper[i][j]
            if i <= j - 1:
                entry = entry + 0.5 * upper[i][j - 1]
            hess[i][j] = entry
    right = [upper[0][0]] + [None] * KB
    for j in range(KB):
        a, b = hess[j][j], hess[j + 1][j]
        inverse = 1.0 / jnp.sqrt(a * a + b * b)
        c, s = a * inverse, b * inverse
        for k in range(j, KB):
            x, y = hess[j][k], hess[j + 1][k]
            if k == j:
                hess[j][k] = c * x + s * y
            else:
                hess[j][k] = c * x + s * y
                hess[j + 1][k] = c * y - s * x
        x = right[j]
        right[j] = c * x
        right[j + 1] = -s * x
    weight = [None] * KB
    for j in range(KB - 1, -1, -1):
        rest = right[j]
        for k in range(j + 1, KB):
            rest = rest - hess[j][k] * weight[k]
        weight[j] = rest / hess[j][j]
    combined = []
    for i in range(n):
        terms = []
        if i < KB:
            terms.append(weight[i])
        if i >= 1:
            terms.append((1.0 if i == 1 else 0.5) * weight[i - 1])
        if i + 1 < KB:
            terms.append(0.5 * weight[i + 1])
        combined.append(functools.reduce(jnp.add, terms))
    return weight, combined


def kernel(
    size_x,
    size_y,
    forcing_ref,
    depth_ref,
    mask_ref,
    agg_ref,
    inverse_ref,
    inverse_smem,
    solution_ref,
    residual_ref,
    in_f,
    in_b,
    in_m,
    wet,
    ocean,
    res,
    sol,
    basis,
    k_south,
    k_north,
    k_east,
    k_west,
    centre,
    send_col,
    got_col,
    send_corner,
    got_corner,
    got_row,
    inverse_rows,
    perm_rows,
    sums,
    factors,
    first_x,
    first_y,
    max_x,
    max_y,
    coarse_x,
    coarse_y,
    gram_x,
    gram_y,
    in_sem,
    halo_send,
    halo_recv,
    phase_send,
    phase_recv,
):
    height = in_f.shape[1]
    own_panels = in_f.shape[0]
    panels = own_panels + 1
    bands = height // TILE
    n_agg = inverse_ref.shape[1]
    rows_all = wet.shape[1]
    group_rows = height // GROUPS
    edge = own_panels
    gx, gy = lax.axis_index("gx"), lax.axis_index("gy")
    first_row = (gx * size_y + gy) * bands

    loads = []
    for index, (source, target) in enumerate(((depth_ref, in_b), (mask_ref, in_m), (forcing_ref, in_f))):
        for p in range(own_panels):
            copy = pltpu.make_async_copy(
                source.at[:, pl.ds(LANES * p, LANES)], target.at[p], in_sem.at[index * own_panels + p]
            )
            copy.start()
            loads.append(copy)
    barrier = pltpu.get_barrier_semaphore()

    def peer_x(d):
        return (lax.rem(gx + d, size_x), gy)

    def peer_y(d):
        return (gx, lax.rem(gy + d, size_y))

    def neighbour(side):
        dx, dy = SIDES[side]
        return (lax.rem(gx + dx + size_x, size_x), lax.rem(gy + dy + size_y, size_y))

    for d in range(1, size_x):
        pl.semaphore_signal(barrier, inc=1, device_id=peer_x(d), device_id_type=MESH)
    for d in range(1, size_y):
        pl.semaphore_signal(barrier, inc=1, device_id=peer_y(d), device_id_type=MESH)
    for side in (NW, NE, SW, SE):
        pl.semaphore_signal(barrier, inc=1, device_id=neighbour(side), device_id_type=MESH)

    sub = lax.broadcasted_iota(jnp.int32, (8, LANES), 0)
    lane8 = lax.broadcasted_iota(jnp.int32, (8, LANES), 1)
    lane16 = lax.broadcasted_iota(jnp.int32, (ROW_STEP, LANES), 1)
    zero8 = jnp.zeros((8, LANES), jnp.float32)

    for p in range(panels):
        for start in (0, rows_all - PAD):
            wet[p, start : start + PAD, :] = zero8

    def clear(j, carry):
        for p in range(panels):
            for start in (0, rows_all - PAD):
                basis[j, p, start : start + PAD, :] = zero8
        return carry

    lax.fori_loop(0, KB + 1, clear, 0)
    sums[...] = jnp.zeros_like(sums)
    inverse_rows[...] = jnp.zeros_like(inverse_rows)
    for s in range(bands):
        for c in range(-(-n_agg // LANES)):
            width = min(LANES, n_agg - c * LANES)
            inverse_rows[s, c : c + 1, 0:width] = inverse_ref[s : s + 1, c * LANES : c * LANES + width]

    for copy in loads:
        copy.wait()

    band_sums = []
    for t in range(bands):

        def prepare(c, total, t=t):
            r = t * TILE + c * ROW_STEP
            for p in range(own_panels):
                rows = pl.ds(r, ROW_STEP)
                at = pl.ds(OWN + r, ROW_STEP)
                sea = in_m[p, rows, :].astype(jnp.float32)
                value = in_f[p, rows, :] * sea
                wet[p, at, :] = in_b[p, rows, :] * sea
                ocean[p, at, :] = sea
                res[p, at, :] = value
                total = total + fold(value * sea)
            return total

        band_sums.append(splat_sum(lax.fori_loop(0, TILE // ROW_STEP, prepare, zero8)))

    def pack(c, carry):
        r = c * ROW_STEP
        for side, p, base in ((WEST, 0, 0), (EAST, own_panels - 1, LANES - DEPTH)):
            packed = jnp.zeros((ROW_STEP, LANES), jnp.float32)
            for g in range(GROUPS):
                at = pl.ds(OWN + g * group_rows + r, ROW_STEP)
                for part, array in enumerate((wet, res)):
                    start = (2 * g + part) * DEPTH
                    moved = pltpu.roll(array[p, at, :], (start - base) % LANES, 1)
                    packed = jnp.where((lane16 >= start) & (lane16 < start + DEPTH), moved, packed)
            send_col[side - WEST, pl.ds(r, ROW_STEP), :] = packed
        return carry

    lax.fori_loop(0, group_rows // ROW_STEP, pack, 0)
    for index, side in enumerate((NW, NE, SW, SE)):
        dx, dy = SIDES[side]
        p, base = (0, 0) if dy < 0 else (own_panels - 1, LANES - DEPTH)
        start = OWN if dx < 0 else OWN + height - DEPTH
        packed = jnp.zeros((DEPTH, LANES), jnp.float32)
        for part, array in enumerate((wet, res)):
            moved = pltpu.roll(array[p, start : start + DEPTH, :], (part * DEPTH - base) % LANES, 1)
            packed = jnp.where((lane16 >= part * DEPTH) & (lane16 < (part + 1) * DEPTH), moved, packed)
        send_corner[index] = packed

    halos = []
    for side in range(8):
        if side in (NORTH, SOUTH):
            start = OWN if side == NORTH else OWN + height - DEPTH
            pairs = [
                (array.at[pl.ds(0, own_panels), pl.ds(start, DEPTH), :], got_row.at[side, part])
                for part, array in enumerate((wet, res))
            ]
        elif side in (WEST, EAST):
            pairs = [(send_col.at[side - WEST], got_col.at[side - WEST])]
        else:
            pairs = [(send_corner.at[side - NW], got_corner.at[side - NW])]
        for part, (source, target) in enumerate(pairs):
            slot = side if part == 0 else 8 + side
            halos.append(
                pltpu.make_async_remote_copy(
                    src_ref=source,
                    dst_ref=target,
                    send_sem=halo_send.at[slot],
                    recv_sem=halo_recv.at[slot],
                    device_id=neighbour(side),
                    device_id_type=MESH,
                )
            )

    def phase(buffer, index, along_x):
        size, me, peer = (size_x, gx, peer_x) if along_x else (size_y, gy, peer_y)

        def start():
            for d in range(1, size):
                pltpu.make_async_remote_copy(
                    src_ref=buffer.at[me],
                    dst_ref=buffer.at[me],
                    send_sem=phase_send.at[index],
                    recv_sem=phase_recv.at[index],
                    device_id=peer(d),
                    device_id_type=MESH,
                ).start()

        def whole():
            part = buffer.at[pl.ds(0, size - 1)]
            return pltpu.make_async_remote_copy(
                src_ref=part,
                dst_ref=part,
                send_sem=phase_send.at[index],
                recv_sem=phase_recv.at[index],
                device_id=peer(1),
                device_id_type=MESH,
            )

        return start, (lambda: whole().wait_recv()), (lambda: whole().wait_send())

    def total_of(buffer, size, *index):
        return functools.reduce(jnp.add, [buffer[(i,) + index] for i in range(size)])

    finish = []

    aggregate = sub * LANES + lane8
    by_aggregate, where_table = zero8, zero8
    for t in range(bands):
        label = agg_ref[t, 0]
        by_aggregate = jnp.where(aggregate == label, band_sums[t], by_aggregate)
        here = (sub == gx) & (lane8 == gy * bands + t)
        where_table = jnp.where(here, (label + 1).astype(jnp.float32), where_table)
    first_x[gx, 0] = by_aggregate
    first_x[gx, 1] = where_table

    pl.semaphore_wait(barrier, size_x + size_y - 2 + 4)
    for copy in halos:
        copy.start()
    start_fx, wait_fx, done_fx = phase(first_x, 0, True)
    start_fy, wait_fy, done_fy = phase(first_y, 1, False)
    start_mx, wait_mx, done_mx = phase(max_x, 2, True)
    start_my, wait_my, done_my = phase(max_y, 3, False)
    finish += [done_fx, done_fy, done_mx, done_my]
    start_fx()
    wait_fx()
    for part in range(2):
        first_y[gy, part] = total_of(first_x, size_x, part)
    start_fy()

    for copy in halos:
        copy.wait()

    east_lanes = jnp.where(gy < size_y - 1, DEPTH, 0)
    west_lane = jnp.where(gy > 0, LANES - DEPTH, LANES)
    for side, start, inside in ((SOUTH, PAD, gx > 0), (NORTH, OWN + height, gx < size_x - 1)):
        keep = jnp.where(inside, LANES, 0)
        for p in range(own_panels):
            depth = jnp.where(lane16 < keep, got_row[side, 0, p], 0.0)
            wet[p, start : start + DEPTH, :] = depth
            res[p, start : start + DEPTH, :] = jnp.where(lane16 < keep, got_row[side, 1, p], 0.0)
            ocean[p, start : start + DEPTH, :] = jnp.where(depth > 0.0, 1.0, 0.0)
        from_east, from_west = (SW, SE) if side == SOUTH else (NW, NE)
        parts = []
        for part in range(2):
            east = pltpu.roll(got_corner[from_east - NW], (-part * DEPTH) % LANES, 1)
            west = pltpu.roll(got_corner[from_west - NW], (-(part + 1) * DEPTH) % LANES, 1)
            value = jnp.where(lane16 < east_lanes, east, jnp.where(lane16 >= west_lane, west, 0.0))
            parts.append(jnp.where(inside, value, 0.0))
        wet[edge, start : start + DEPTH, :] = parts[0]
        res[edge, start : start + DEPTH, :] = parts[1]
        ocean[edge, start : start + DEPTH, :] = jnp.where(parts[0] > 0.0, 1.0, 0.0)

    def unpack(c, carry):
        r = c * ROW_STEP
        east_all = got_col[WEST - WEST, pl.ds(r, ROW_STEP), :]
        west_all = got_col[EAST - WEST, pl.ds(r, ROW_STEP), :]
        for g in range(GROUPS):
            at = pl.ds(OWN + g * group_rows + r, ROW_STEP)
            parts = []
            for part in range(2):
                start = (2 * g + part) * DEPTH
                east = pltpu.roll(east_all, (-start) % LANES, 1)
                west = pltpu.roll(west_all, (LANES - DEPTH - start) % LANES, 1)
                parts.append(
                    jnp.where(lane16 < east_lanes, east, jnp.where(lane16 >= west_lane, west, 0.0))
                )
            wet[edge, at, :] = parts[0]
            res[edge, at, :] = parts[1]
            ocean[edge, at, :] = jnp.where(parts[0] > 0.0, 1.0, 0.0)
        return carry

    lax.fori_loop(0, group_rows // ROW_STEP, unpack, 0)

    def east_west(values):
        left = [pltpu.roll(v, LANES - 1, 1) for v in values]
        right = [pltpu.roll(v, 1, 1) for v in values]
        easts = [jnp.where(lane16 == LANES - 1, left[(p + 1) % panels], left[p]) for p in range(panels)]
        wests = [jnp.where(lane16 == 0, right[p - 1], right[p]) for p in range(panels)]
        return easts, wests

    def faces(r, top):
        values = [wet[p, pl.ds(r, ROW_STEP), :] for p in range(panels)]
        easts, wests = east_west(values)
        for p in range(panels):
            at = pl.ds(r, ROW_STEP)
            south = jnp.minimum(values[p], wet[p, pl.ds(r + 1, ROW_STEP), :])
            north = jnp.minimum(values[p], wet[p, pl.ds(r - 1, ROW_STEP), :])
            east = jnp.minimum(values[p], easts[p])
            west = jnp.minimum(values[p], wests[p])
            k_south[p, at, :] = south
            k_north[p, at, :] = north
            k_east[p, at, :] = east
            k_west[p, at, :] = west
            diagonal = 1.0 + south + north + east + west
            centre[p, at, :] = diagonal
            if p < own_panels and top is not None:
                for start in range(0, ROW_STEP, 8):
                    top = jnp.maximum(top, diagonal[start : start + 8])
        return top

    top = lax.fori_loop(
        0, height // ROW_STEP, lambda c, top: faces(OWN + c * ROW_STEP, top), jnp.ones((8, LANES), jnp.float32)
    )
    max_x[gx] = top
    start_mx()
    faces(PAD, None)
    faces(OWN + height, None)

    wait_fy()
    rhs = total_of(first_y, size_y, 0)
    table = total_of(first_y, size_y, 1).astype(jnp.int32) - 1

    def spread_coarse(rhs, rows, buffer):
        tile = zero8
        for s in range(bands):
            tile = jnp.where(table == first_row + s, splat_sum(rows[s] * rhs), tile)
        buffer[gx] = tile

    spread_coarse(rhs, inverse_rows, coarse_x.at[0])
    starts = [phase(coarse_x.at[c], 4 + 2 * c, True) for c in range(CYCLES)]
    starts_y = [phase(coarse_y.at[c], 5 + 2 * c, False) for c in range(CYCLES)]
    finish += [s[2] for s in starts] + [s[2] for s in starts_y]
    starts[0][0]()

    wait_mx()
    max_y[gy] = functools.reduce(jnp.maximum, [max_x[i] for i in range(size_x)])
    start_my()

    def permute(q, carry):
        match = table == q
        return tuple(jnp.where(match, inverse_smem[s, q], carry[s]) for s in range(bands))

    permuted = lax.fori_loop(0, n_agg, permute, (zero8,) * bands, unroll=8)
    for s in range(bands):
        perm_rows[s] = permuted[s]

    starts[0][1]()
    coarse_y[0, gy] = total_of(coarse_x.at[0], size_x)
    starts_y[0][0]()
    wait_my()
    largest = functools.reduce(jnp.maximum, [max_y[i] for i in range(size_y)])
    for move in (4, 2, 1):
        largest = jnp.maximum(largest, pltpu.roll(largest, move, 0))
    shift = jnp.broadcast_to(jnp.max(largest, axis=1, keepdims=True), (8, LANES))
    scale = 2.0 / shift
    scale16 = tall(scale, ROW_STEP)

    def rescale(c, carry):
        at = pl.ds(PAD + c * ROW_STEP, ROW_STEP)
        for p in range(panels):
            for array in (k_south, k_north, k_east, k_west):
                array[p, at, :] = array[p, at, :] * scale16
            centre[p, at, :] = centre[p, at, :] * scale16 - 2.0
        return carry

    chunks_all = (rows_all - 2 * PAD) // ROW_STEP
    lax.fori_loop(0, chunks_all, rescale, 0)

    def stencil(index, r):
        at = pl.ds(r, ROW_STEP)
        values = [basis[index, p, at, :] for p in range(panels)]
        easts, wests = east_west(values)
        out = []
        for p in range(panels):
            south = basis[index, p, pl.ds(r + 1, ROW_STEP), :]
            north = basis[index, p, pl.ds(r - 1, ROW_STEP), :]
            flow = k_south[p, at, :] * south + k_north[p, at, :] * north
            flow = flow + (k_east[p, at, :] * easts[p] + k_west[p, at, :] * wests[p])
            out.append(centre[p, at, :] * values[p] - flow)
        return out, values

    shift16 = tall(shift, ROW_STEP)
    gram_phases = [(phase(gram_x.at[c], 8 + 2 * c, True), phase(gram_y.at[c], 9 + 2 * c, False)) for c in range(CYCLES)]
    finish += [p[2] for pair in gram_phases for p in pair]

    for cycle in range(CYCLES):
        starts_y[cycle][1]()
        tile = total_of(coarse_y.at[cycle], size_y)
        rows_of = {dx: sub_total(jnp.where(sub == gx + dx, tile, 0.0)) for dx in (-1, 0, 1)}

        def value_at(dx, t, dy):
            picked = jnp.where(lane8 == (gy + dy) * bands + t, rows_of[dx], 0.0)
            return jnp.broadcast_to(jnp.sum(picked, axis=1, keepdims=True), (8, LANES))

        def spread_band(dx, t, start, chunks):
            own = tall(value_at(dx, t, 0), ROW_STEP)
            side = tall(jnp.where(lane8 < LANES // 2, value_at(dx, t, 1), value_at(dx, t, -1)), ROW_STEP)

            def body(c, carry):
                at = pl.ds(start + c * ROW_STEP, ROW_STEP)
                for p in range(panels):
                    value = ocean[p, at, :] * (side if p == edge else own)
                    basis[KB, p, at, :] = value
                    if dx == 0 and p < own_panels:
                        inner = pl.ds(start - OWN + c * ROW_STEP, ROW_STEP)
                        sol[p, inner, :] = value if cycle == 0 else sol[p, inner, :] + value
                return carry

            lax.fori_loop(0, chunks, body, 0)

        spread_band(-1, bands - 1, PAD, DEPTH // ROW_STEP)
        for t in range(bands):
            spread_band(0, t, OWN + t * TILE, TILE // ROW_STEP)
        spread_band(1, 0, OWN + height, DEPTH // ROW_STEP)

        def first(r, carry):
            out, values = stencil(KB, r)
            at = pl.ds(r, ROW_STEP)
            for p in range(panels):
                v = res[p, at, :] - shift16 * (0.5 * out[p] + values[p])
                basis[0, p, at, :] = v
                if p < own_panels and carry is not None:
                    square, total = carry
                    carry = (square + fold(v * v), total + fold(v * ocean[p, at, :]))
            return carry

        first(PAD, None)
        first(OWN + height, None)
        square = zero8
        for t in range(bands):
            square, total = lax.fori_loop(
                0,
                TILE // ROW_STEP,
                lambda c, carry, t=t: first(OWN + t * TILE + c * ROW_STEP, carry),
                (square, zero8),
            )
            sums[t : t + 1, :] = jnp.sum(total, axis=0, keepdims=True)
        sums[64:65, :] = jnp.sum(square, axis=0, keepdims=True)

        def step(j, carry):
            previous = jnp.maximum(j - 2, 0)
            new_part = jnp.where(j == 1, 0.5, 1.0)
            old_part = jnp.where(j == 1, 0.0, 1.0)

            def chunk(r, carry):
                out, values = stencil(j - 1, r)
                at = pl.ds(r, ROW_STEP)
                for p in range(panels):
                    v = new_part * out[p] - old_part * basis[previous, p, at, :]
                    basis[j, p, at, :] = v
                    if p < own_panels and carry is not None:
                        square, cross, total = carry
                        carry = (
                            square + fold(v * v),
                            cross + fold(v * values[p]),
                            total + fold(v * ocean[p, at, :]),
                        )
                return carry

            chunk(PAD, None)
            chunk(OWN + height, None)
            square, cross = zero8, zero8
            for t in range(bands):
                square, cross, total = lax.fori_loop(
                    0,
                    TILE // ROW_STEP,
                    lambda c, carry, t=t: chunk(OWN + t * TILE + c * ROW_STEP, carry),
                    (square, cross, zero8),
                )
                sums[pl.ds(j * bands + t, 1), :] = jnp.sum(total, axis=0, keepdims=True)
            sums[pl.ds(64 + j, 1), :] = jnp.sum(square, axis=0, keepdims=True)
            sums[pl.ds(80 + j, 1), :] = jnp.sum(cross, axis=0, keepdims=True)
            return carry

        lax.fori_loop(1, KB + 1, step, 0)

        row = lax.dot_general(
            jnp.ones((8, LANES), jnp.float32),
            sums[...],
            (((1,), (1,)), ((), ())),
            precision=highest,
            preferred_element_type=jnp.float32,
        )
        (start_gx, wait_gx, _), (start_gy, wait_gy, _) = gram_phases[cycle]
        gram_x[cycle, gx] = jnp.where(sub == gx, row, 0.0)
        start_gx()
        wait_gx()
        gram_y[cycle, gy] = total_of(gram_x.at[cycle], size_x)
        start_gy()
        wait_gy()
        gathered = [gram_y[cycle, i] for i in range(size_y)]
        whole = sub_total(functools.reduce(jnp.add, gathered))

        def at_lane(k):
            return jnp.broadcast_to(whole[:, k : k + 1], (8, LANES))

        vv = [at_lane(64 + a) for a in range(KB + 1)]
        vp = [None] + [at_lane(80 + a) for a in range(1, KB + 1)]
        weight, combined = small_solve(vv, vp)
        for j in range(KB):
            factors[j] = weight[j] / shift
        for a in range(KB + 1):
            factors[KB + a] = combined[a]

        if cycle < CYCLES - 1:
            group = lane8 // bands
            mix = jnp.where(group == 0, 1.0, 0.0)
            for a in range(KB + 1):
                mix = jnp.where(group == a, mix - combined[a], mix)
            rhs = zero8
            for i in range(size_y):
                part = gathered[i] * jnp.where(lane8 < (KB + 1) * bands, mix, 0.0)
                move = bands
                while move < LANES:
                    part = part + pltpu.roll(part, move, 1)
                    move *= 2
                rhs = jnp.where(group == i, part, rhs)
            spread_coarse(rhs, perm_rows, coarse_x.at[cycle + 1])
            starts[cycle + 1][0]()

        w = [tall(factors[j], ROW_STEP) for j in range(KB)]
        c_all = [tall(factors[KB + a], ROW_STEP) for a in range(KB + 1)]

        def update(r, p, inner):
            at = pl.ds(r, ROW_STEP)
            values = [basis[a, p, at, :] for a in range(KB + 1)]
            residual = values[0]
            for a in range(KB + 1):
                residual = residual - c_all[a] * values[a]
            if inner is None:
                res[p, at, :] = residual
                return
            rows = pl.ds(inner, ROW_STEP)
            answer = sol[p, rows, :]
            for j in range(KB):
                answer = answer + w[j] * values[j]
            if cycle < CYCLES - 1:
                res[p, at, :] = residual
                sol[p, rows, :] = answer
            else:
                columns = pl.ds(p * LANES, LANES)
                residual_ref[rows, columns] = residual
                solution_ref[rows, columns] = answer

        def update_own(c, carry):
            for p in range(own_panels):
                update(OWN + c * ROW_STEP, p, c * ROW_STEP)
            if cycle < CYCLES - 1:
                update(OWN + c * ROW_STEP, edge, None)
            return carry

        lax.fori_loop(0, height // ROW_STEP, update_own, 0)
        if cycle < CYCLES - 1:
            for p in range(panels):
                update(PAD, p, None)
                update(OWN + height, p, None)
            starts[cycle + 1][1]()
            coarse_y[cycle + 1, gy] = total_of(coarse_x.at[cycle + 1], size_x)
            starts_y[cycle + 1][0]()

    for done in finish:
        done()


def on_device(size_x, size_y, forcing, bathymetry, ocean_mask, aggregate_id, coarse_inverse):
    height, breadth = forcing.shape
    own_panels = breadth // LANES
    panels = own_panels + 1
    rows = height + 2 * (DEPTH + PAD)
    bands = height // TILE
    f32 = jnp.float32
    field = pltpu.VMEM((panels, rows, LANES), f32)
    block = pltpu.VMEM((own_panels, height, LANES), f32)
    any_spec = pl.BlockSpec(memory_space=pl.ANY)
    vmem = pl.BlockSpec(memory_space=pltpu.VMEM)
    smem = pl.BlockSpec(memory_space=pltpu.SMEM)
    tiles = lambda *lead: pltpu.VMEM(lead + (8, LANES), f32)
    dma = pltpu.SemaphoreType.DMA
    return pl.pallas_call(
        functools.partial(kernel, size_x, size_y),
        out_shape=(jax.ShapeDtypeStruct((height, breadth), f32),) * 2,
        in_specs=[any_spec, any_spec, any_spec, smem, vmem, smem],
        out_specs=(vmem, vmem),
        scratch_shapes=[
            block,
            block,
            pltpu.VMEM((own_panels, height, LANES), jnp.int32),
            field,
            field,
            field,
            block,
            pltpu.VMEM((KB + 1, panels, rows, LANES), f32),
            field,
            field,
            field,
            field,
            field,
            pltpu.VMEM((2, height // GROUPS, LANES), f32),
            pltpu.VMEM((2, height // GROUPS, LANES), f32),
            pltpu.VMEM((4, DEPTH, LANES), f32),
            pltpu.VMEM((4, DEPTH, LANES), f32),
            pltpu.VMEM((2, 2, own_panels, DEPTH, LANES), f32),
            tiles(bands),
            tiles(bands),
            pltpu.VMEM((LANES, LANES), f32),
            tiles(2 * KB + 1),
            tiles(size_x, 2),
            tiles(size_y, 2),
            tiles(size_x),
            tiles(size_y),
            tiles(CYCLES, size_x),
            tiles(CYCLES, size_y),
            tiles(CYCLES, size_x),
            tiles(CYCLES, size_y),
            dma((3 * own_panels,)),
            dma((10,)),
            dma((10,)),
            dma((12,)),
            dma((12,)),
        ],
        compiler_params=pltpu.CompilerParams(
            collective_id=0, has_side_effects=True, vmem_limit_bytes=48 * 1024 * 1024
        ),
    )(forcing, bathymetry, ocean_mask, aggregate_id, coarse_inverse, coarse_inverse)


def solution(mesh):
    return jax.shard_map(
        functools.partial(on_device, mesh.shape["gx"], mesh.shape["gy"]),
        mesh=mesh,
        in_specs=(
            P("gx", "gy"),
            P("gx", "gy"),
            P("gx", "gy"),
            P("gx", "gy"),
            P(("gx", "gy"), None),
        ),
        out_specs=(P("gx", "gy"), P("gx", "gy")),
        check_vma=False,
    )
```

time: 1160 us -> 98.1 us (0.08); the launches traced: 1140 us -> 97.8 us
  blocking collectives: 332 us -> 0 us
  starting transfers between devices: 199 us -> 0 us
  local copies, waits for them, and re-layouts: 188 us -> 6.08 us
  matrix products: 138 us -> 0 us
  waiting for transfers between devices: 107 us -> 0 us
  other arithmetic: 95.1 us -> 0 us
  Pallas kernels: 0 us -> 91 us
  between operations: 77.9 us -> 0.65 us
    psum x4 -> x0, blocking collectives: 266 us -> none  [the longest x2 136 us: on_device(): gram = lax.psum(gram_local, ('gx', 'gy'))]
    ppermute x76 -> x0, starting transfers between devices: 199 us -> none  [the longest x38 137 us: padded_2(): lax.ppermute(tail, axis, [(i, (i + 1) % count) for i in range(ends)])]
    dot_general x72 -> x0, matrix products: 138 us -> none  [the longest x24 47.3 us: small_solve(): amounts = jnp.dot(earlier_cols.T, vector, precision=highest)]
    ppermute x76 -> x0, waiting for transfers between devices: 107 us -> none  [the longest x38 96.8 us: padded_2(): lax.ppermute(head, axis, [((i + 1) % count, i) for i in range(ends)])]
    pallas_call x0 -> x1, Pallas kernels: none -> 91 us  [on_device(): pl.pallas_call(functools.partial(kernel, size_x, size_y), out_shape=(jax....]
    another operation x26 -> x0, local copies, waits for them, and re-layouts: 77.2 us -> none  [the longest x4 65.3 us: on_device(): fields = jnp.stack(krylov)]
    pmax x1 -> x0, blocking collectives: 66 us -> none  [on_device(): spectral_shift = lax.pmax(jnp.max(diagonal), ('gx', 'gy'))]
    scatter-add x28 -> x0, local copies, waits for them, and re-layouts: 40.8 us -> none  [small_solve(): triangle = triangle.at[:column, column].add(amounts)]
  transfers between devices with their start and end apart: 77 -> 0, of which waited for: 43 -> 0; matrix products, arithmetic and copies ran while one was open for 6% -> 0% of each run, Pallas kernels for 0% -> 0%
where the time goes in v1:
time: 98.1 us; the launch traced here: 97.8 us
  Pallas kernels  91 us (93%)
  local copies, waits for them, and re-layouts  6.08 us (6%)
    pallas_call x1, Pallas kernels, on_device(): pl.pallas_call(functools.partial(kernel, size_x, size_y), out_shape=(jax....  91 us
    unnamed x12, local copies, waits for them, and re-layouts  6.08 us

profile of v1, /device:TPU:1, one launch (start us, length us, event | category | flops | bytes accessed | tf_op | source)
XLA Modules:
  0.0 97.8 jit_solution(5102660586929861312)
XLA Ops:
  0.6 0.0 copy-start
  0.6 1.0 %copy-done = f32[256,512]{1,0:T(8,128)S(1)} copy-done((f32[256,512]{1,0:T(8,128)S(1)}, f32[256,512]{1,0:T(8,128)}, u32[]{:S(2)}) %copy-start) | copy-done | bytes 524312
  1.7 0.0 copy-start.1
  1.7 1.0 %copy-done.1 = f32[256,512]{1,0:T(8,128)S(1)} copy-done((f32[256,512]{1,0:T(8,128)S(1)}, f32[256,512]{1,0:T(8,128)}, u32[]{:S(2)}) %copy-start.1) | copy-done | bytes 524312
  2.7 0.0 copy-start.2
  2.7 1.0 %copy-done.2 = s32[256,512]{1,0:T(8,128)S(1)} copy-done((s32[256,512]{1,0:T(8,128)S(1)}, s32[256,512]{1,0:T(8,128)}, u32[]{:S(2)}) %copy-start.2) | copy-done | bytes 524312
  3.8 0.0 copy-start.3
  3.8 0.7 copy-done.3
  4.5 0.0 copy-start.4
  4.5 0.7 copy-done.4
  5.1 91.0 %shard_map.68 = (f32[256,512]{1,0:T(8,128)S(1)}, f32[256,512]{1,0:T(8,128)S(1)}) custom-call(f32[256,512]{1,0:T(8,128)S(1)} %copy-done, f32[256,512]{1,0:T(8,128)S(1)} %copy-done.1, s32[256,512]{1,0:T(8,128)S(1)} %copy-done.2, s32[4,8]{1,0:T(4,128)S(1)} %copy-done.4, f32[4,512]{1,0:T(4,128)S(1)} %copy-done.3, f32[4,512]{1,0:T(4,128)S(1)} %copy-done.3), custom_call_target="tpu_custom_call" | custom-call | tf_op jit(solution)/shard_map/pallas_call | solution.py:688
  96.2 0.8 copy.9
  97.0 0.8 copy.10
Async XLA Ops:
  0.6 1.0 %copy-start = (f32[256,512]{1,0:T(8,128)S(1)}, f32[256,512]{1,0:T(8,128)}, u32[]{:S(2)}) copy-start(f32[256,512]{1,0:T(8,128)} %forcing_ref.1) | copy-start | bytes 1572868
  1.7 1.0 %copy-start.1 = (f32[256,512]{1,0:T(8,128)S(1)}, f32[256,512]{1,0:T(8,128)}, u32[]{:S(2)}) copy-start(f32[256,512]{1,0:T(8,128)} %depth_ref.1) | copy-start | bytes 1572868
  2.7 1.0 %copy-start.2 = (s32[256,512]{1,0:T(8,128)S(1)}, s32[256,512]{1,0:T(8,128)}, u32[]{:S(2)}) copy-start(s32[256,512]{1,0:T(8,128)} %mask_ref.1) | copy-start | bytes 1572868
  3.8 0.7 copy-start.3
  4.5 0.7 copy-start.4

commit v2 on v1

--- a/solution.py
+++ b/solution.py
@@ -17,6 +17,7 @@
 OWN = PAD + DEPTH
 ROW_STEP = 16
 GROUPS = 4
+FIRST = 20
 MESH = pl.DeviceIdType.MESH
 highest = lax.Precision.HIGHEST
 SIDES = ((-1, 0), (1, 0), (0, -1), (0, 1), (-1, -1), (-1, 1), (1, -1), (1, 1))
@@ -42,6 +43,18 @@
 
 def tall(x, rows):
     return jnp.concatenate([x] * (rows // 8), axis=0)
+
+
+def split(x):
+    high = x.astype(jnp.bfloat16)
+    return high, (x - high.astype(jnp.float32)).astype(jnp.bfloat16)
+
+
+def placed(x, chooser):
+    high, low = split(x)
+    return jnp.dot(high, chooser, preferred_element_type=jnp.float32) + jnp.dot(
+        low, chooser, preferred_element_type=jnp.float32
+    )
 
 
 def small_solve(vv, vp):
@@ -126,11 +139,17 @@
     in_f,
     in_b,
     in_m,
+    side_w,
+    side_r,
+    chooser,
+    back,
     wet,
     ocean,
     res,
     sol,
     basis,
+    even,
+    odd,
     k_south,
     k_north,
     k_east,
@@ -159,25 +178,21 @@
     phase_send,
     phase_recv,
 ):
-    height = in_f.shape[1]
-    own_panels = in_f.shape[0]
+    height, breadth = in_f.shape
+    own_panels = breadth // LANES
     panels = own_panels + 1
     bands = height // TILE
     n_agg = inverse_ref.shape[1]
     rows_all = wet.shape[1]
     group_rows = height // GROUPS
-    edge = own_panels
     gx, gy = lax.axis_index("gx"), lax.axis_index("gy")
     first_row = (gx * size_y + gy) * bands
 
     loads = []
     for index, (source, target) in enumerate(((depth_ref, in_b), (mask_ref, in_m), (forcing_ref, in_f))):
-        for p in range(own_panels):
-            copy = pltpu.make_async_copy(
-                source.at[:, pl.ds(LANES * p, LANES)], target.at[p], in_sem.at[index * own_panels + p]
-            )
-            copy.start()
-            loads.append(copy)
+        copy = pltpu.make_async_copy(source, target, in_sem.at[index])
+        copy.start()
+        loads.append(copy)
     barrier = pltpu.get_barrier_semaphore()
 
     def peer_x(d):
@@ -204,15 +219,8 @@
 
     for p in range(panels):
         for start in (0, rows_all - PAD):
-            wet[p, start : start + PAD, :] = zero8
-
-    def clear(j, carry):
-        for p in range(panels):
-            for start in (0, rows_all - PAD):
-                basis[j, p, start : start + PAD, :] = zero8
-        return carry
-
-    lax.fori_loop(0, KB + 1, clear, 0)
+            for array in (wet, even, odd):
+                array[p, start : start + PAD, :] = zero8
     sums[...] = jnp.zeros_like(sums)
     inverse_rows[...] = jnp.zeros_like(inverse_rows)
     for s in range(bands):
@@ -220,6 +228,22 @@
             width = min(LANES, n_agg - c * LANES)
             inverse_rows[s, c : c + 1, 0:width] = inverse_ref[s : s + 1, c * LANES : c * LANES + width]
 
+    def place(rows, columns, column_base, transposed):
+        line = lax.broadcasted_iota(jnp.int32, (rows, columns), 1 if transposed else 0) + column_base
+        spot = lax.broadcasted_iota(jnp.int32, (rows, columns), 0 if transposed else 1)
+        return jnp.where(line < breadth + LANES // 2, line, line - panels * LANES) + FIRST, spot
+
+    def choose(c, carry):
+        rows = pl.ds(c * 16, 16)
+        for p in range(panels):
+            goal, lane = place(16, LANES, c * 16, False)
+            chooser[rows, p * LANES : (p + 1) * LANES] = jnp.where(goal == lane * panels + p, 1.0, 0.0).astype(
+                jnp.bfloat16
+            )
+        return carry
+
+    lax.fori_loop(0, panels * LANES // 16, choose, 0)
+
     for copy in loads:
         copy.wait()
 
@@ -227,15 +251,13 @@
     for t in range(bands):
 
         def prepare(c, total, t=t):
-            r = t * TILE + c * ROW_STEP
+            rows = pl.ds(t * TILE + c * ROW_STEP, ROW_STEP)
             for p in range(own_panels):
-                rows = pl.ds(r, ROW_STEP)
-                at = pl.ds(OWN + r, ROW_STEP)
-                sea = in_m[p, rows, :].astype(jnp.float32)
-                value = in_f[p, rows, :] * sea
-                wet[p, at, :] = in_b[p, rows, :] * sea
-                ocean[p, at, :] = sea
-                res[p, at, :] = value
+                at = pl.ds(p * LANES, LANES)
+                sea = in_m[rows, at].astype(jnp.float32)
+                value = in_f[rows, at] * sea
+                in_b[rows, at] = in_b[rows, at] * sea
+                in_f[rows, at] = value
                 total = total + fold(value * sea)
             return total
 
@@ -246,10 +268,10 @@
         for side, p, base in ((WEST, 0, 0), (EAST, own_panels - 1, LANES - DEPTH)):
             packed = jnp.zeros((ROW_STEP, LANES), jnp.float32)
             for g in range(GROUPS):
-                at = pl.ds(OWN + g * group_rows + r, ROW_STEP)
-                for part, array in enumerate((wet, res)):
+                at = pl.ds(g * group_rows + r, ROW_STEP)
+                for part, array in enumerate((in_b, in_f)):
                     start = (2 * g + part) * DEPTH
-                    moved = pltpu.roll(array[p, at, :], (start - base) % LANES, 1)
+                    moved = pltpu.roll(array[at, p * LANES : (p + 1) * LANES], (start - base) % LANES, 1)
                     packed = jnp.where((lane16 >= start) & (lane16 < start + DEPTH), moved, packed)
             send_col[side - WEST, pl.ds(r, ROW_STEP), :] = packed
         return carry
@@ -258,20 +280,20 @@
     for index, side in enumerate((NW, NE, SW, SE)):
         dx, dy = SIDES[side]
         p, base = (0, 0) if dy < 0 else (own_panels - 1, LANES - DEPTH)
-        start = OWN if dx < 0 else OWN + height - DEPTH
+        start = 0 if dx < 0 else height - DEPTH
         packed = jnp.zeros((DEPTH, LANES), jnp.float32)
-        for part, array in enumerate((wet, res)):
-            moved = pltpu.roll(array[p, start : start + DEPTH, :], (part * DEPTH - base) % LANES, 1)
+        for part, array in enumerate((in_b, in_f)):
+            corner = array[start : start + DEPTH, p * LANES : (p + 1) * LANES]
+            moved = pltpu.roll(corner, (part * DEPTH - base) % LANES, 1)
             packed = jnp.where((lane16 >= part * DEPTH) & (lane16 < (part + 1) * DEPTH), moved, packed)
         send_corner[index] = packed
 
     halos = []
     for side in range(8):
         if side in (NORTH, SOUTH):
-            start = OWN if side == NORTH else OWN + height - DEPTH
+            start = 0 if side == NORTH else height - DEPTH
             pairs = [
-                (array.at[pl.ds(0, own_panels), pl.ds(start, DEPTH), :], got_row.at[side, part])
-                for part, array in enumerate((wet, res))
+                (array.at[pl.ds(start, DEPTH), :], got_row.at[side, part]) for part, array in enumerate((in_b, in_f))
             ]
         elif side in (WEST, EAST):
             pairs = [(send_col.at[side - WEST], got_col.at[side - WEST])]
@@ -341,6 +363,20 @@
     start_my, wait_my, done_my = phase(max_y, 3, False)
     finish += [done_fx, done_fy, done_mx, done_my]
     start_fx()
+
+    own_rows = pl.ds(0, breadth)
+    block_rows = 64
+
+    def settle(c, carry):
+        rows = pl.ds(c * block_rows, block_rows)
+        for source, target in ((in_b, wet), (in_f, res)):
+            moved = placed(source[rows, :], chooser[own_rows, :])
+            for p in range(panels):
+                target[p, pl.ds(OWN + c * block_rows, block_rows), :] = moved[:, p * LANES : (p + 1) * LANES]
+        return carry
+
+    lax.fori_loop(0, height // block_rows, settle, 0)
+
     wait_fx()
     for part in range(2):
         first_y[gy, part] = total_of(first_x, size_x, part)
@@ -352,50 +388,67 @@
     east_lanes = jnp.where(gy < size_y - 1, DEPTH, 0)
     west_lane = jnp.where(gy > 0, LANES - DEPTH, LANES)
     for side, start, inside in ((SOUTH, PAD, gx > 0), (NORTH, OWN + height, gx < size_x - 1)):
-        keep = jnp.where(inside, LANES, 0)
-        for p in range(own_panels):
-            depth = jnp.where(lane16 < keep, got_row[side, 0, p], 0.0)
-            wet[p, start : start + DEPTH, :] = depth
-            res[p, start : start + DEPTH, :] = jnp.where(lane16 < keep, got_row[side, 1, p], 0.0)
-            ocean[p, start : start + DEPTH, :] = jnp.where(depth > 0.0, 1.0, 0.0)
         from_east, from_west = (SW, SE) if side == SOUTH else (NW, NE)
-        parts = []
-        for part in range(2):
+        for part, target in enumerate((wet, res)):
             east = pltpu.roll(got_corner[from_east - NW], (-part * DEPTH) % LANES, 1)
             west = pltpu.roll(got_corner[from_west - NW], (-(part + 1) * DEPTH) % LANES, 1)
-            value = jnp.where(lane16 < east_lanes, east, jnp.where(lane16 >= west_lane, west, 0.0))
-            parts.append(jnp.where(inside, value, 0.0))
-        wet[edge, start : start + DEPTH, :] = parts[0]
-        res[edge, start : start + DEPTH, :] = parts[1]
-        ocean[edge, start : start + DEPTH, :] = jnp.where(parts[0] > 0.0, 1.0, 0.0)
+            corner = jnp.where(lane16 < east_lanes, east, jnp.where(lane16 >= west_lane, west, 0.0))
+            whole_row = jnp.concatenate([got_row[side, part], corner], axis=1)
+            moved = placed(jnp.where(inside, whole_row, 0.0), chooser[...])
+            for p in range(panels):
+                target[p, start : start + DEPTH, :] = moved[:, p * LANES : (p + 1) * LANES]
 
     def unpack(c, carry):
         r = c * ROW_STEP
         east_all = got_col[WEST - WEST, pl.ds(r, ROW_STEP), :]
         west_all = got_col[EAST - WEST, pl.ds(r, ROW_STEP), :]
         for g in range(GROUPS):
-            at = pl.ds(OWN + g * group_rows + r, ROW_STEP)
-            parts = []
-            for part in range(2):
+            for part, target in enumerate((side_w, side_r)):
                 start = (2 * g + part) * DEPTH
                 east = pltpu.roll(east_all, (-start) % LANES, 1)
                 west = pltpu.roll(west_all, (LANES - DEPTH - start) % LANES, 1)
-                parts.append(
-                    jnp.where(lane16 < east_lanes, east, jnp.where(lane16 >= west_lane, west, 0.0))
+                target[pl.ds(g * group_rows + r, ROW_STEP), :] = jnp.where(
+                    lane16 < east_lanes, east, jnp.where(lane16 >= west_lane, west, 0.0)
                 )
-            wet[edge, at, :] = parts[0]
-            res[edge, at, :] = parts[1]
-            ocean[edge, at, :] = jnp.where(parts[0] > 0.0, 1.0, 0.0)
         return carry
 
     lax.fori_loop(0, group_rows // ROW_STEP, unpack, 0)
 
+    def settle_sides(c, carry):
+        rows = pl.ds(c * block_rows, block_rows)
+        at = pl.ds(OWN + c * block_rows, block_rows)
+        for source, target in ((side_w, wet), (side_r, res)):
+            moved = placed(source[rows, :], chooser[pl.ds(breadth, LANES), :])
+            for p in range(panels):
+                target[p, at, :] = target[p, at, :] + moved[:, p * LANES : (p + 1) * LANES]
+        return carry
+
+    lax.fori_loop(0, height // block_rows, settle_sides, 0)
+
     def east_west(values):
-        left = [pltpu.roll(v, LANES - 1, 1) for v in values]
-        right = [pltpu.roll(v, 1, 1) for v in values]
-        easts = [jnp.where(lane16 == LANES - 1, left[(p + 1) % panels], left[p]) for p in range(panels)]
-        wests = [jnp.where(lane16 == 0, right[p - 1], right[p]) for p in range(panels)]
+        easts = values[1:] + [pltpu.roll(values[0], LANES - 1, 1)]
+        wests = [pltpu.roll(values[-1], 1, 1)] + values[:-1]
         return easts, wests
+
+    last, extra = divmod(breadth + FIRST, panels)
+    first_lane = FIRST // panels
+
+    def own_lanes(x, p):
+        lane = lax.broadcasted_iota(jnp.int32, x.shape, 1)
+        return (lane >= first_lane) & (lane < last + (1 if p < extra else 0))
+
+    def kind(p):
+        return 0 if p < extra else 1
+
+    def own_total(parts):
+        return jnp.where(own_lanes(parts[0], 0), parts[0], 0.0) + jnp.where(
+            own_lanes(parts[1], panels - 1), parts[1], 0.0
+        )
+
+    def add_to(pair, p, x):
+        return tuple(total + x if i == kind(p) else total for i, total in enumerate(pair))
+
+    zero_pair = (zero8, zero8)
 
     def faces(r, top):
         values = [wet[p, pl.ds(r, ROW_STEP), :] for p in range(panels)]
@@ -412,15 +465,19 @@
             k_west[p, at, :] = west
             diagonal = 1.0 + south + north + east + west
             centre[p, at, :] = diagonal
-            if p < own_panels and top is not None:
+            ocean[p, at, :] = jnp.where(values[p] > 0.0, 1.0, 0.0)
+            if top is not None:
                 for start in range(0, ROW_STEP, 8):
-                    top = jnp.maximum(top, diagonal[start : start + 8])
+                    part = diagonal[start : start + 8]
+                    top = tuple(jnp.maximum(t, part) if i == kind(p) else t for i, t in enumerate(top))
         return top
 
     top = lax.fori_loop(
-        0, height // ROW_STEP, lambda c, top: faces(OWN + c * ROW_STEP, top), jnp.ones((8, LANES), jnp.float32)
+        0, height // ROW_STEP, lambda c, top: faces(OWN + c * ROW_STEP, top), (jnp.ones((8, LANES), jnp.float32),) * 2
     )
-    max_x[gx] = top
+    max_x[gx] = jnp.maximum(
+        jnp.where(own_lanes(top[0], 0), top[0], 1.0), jnp.where(own_lanes(top[1], panels - 1), top[1], 1.0)
+    )
     start_mx()
     faces(PAD, None)
     faces(OWN + height, None)
@@ -475,19 +532,32 @@
     chunks_all = (rows_all - 2 * PAD) // ROW_STEP
     lax.fori_loop(0, chunks_all, rescale, 0)
 
-    def stencil(index, r):
+    def stencil(array, r):
         at = pl.ds(r, ROW_STEP)
-        values = [basis[index, p, at, :] for p in range(panels)]
+        values = [array[p, at, :] for p in range(panels)]
         easts, wests = east_west(values)
         out = []
         for p in range(panels):
-            south = basis[index, p, pl.ds(r + 1, ROW_STEP), :]
-            north = basis[index, p, pl.ds(r - 1, ROW_STEP), :]
+            south = array[p, pl.ds(r + 1, ROW_STEP), :]
+            north = array[p, pl.ds(r - 1, ROW_STEP), :]
             flow = k_south[p, at, :] * south + k_north[p, at, :] * north
             flow = flow + (k_east[p, at, :] * easts[p] + k_west[p, at, :] * wests[p])
             out.append(centre[p, at, :] * values[p] - flow)
         return out, values
 
+    def over_bands(chunk, first_sums, run):
+        chunk(PAD, None)
+        chunk(OWN + height, None)
+
+        def band(t, carry):
+            carry = carry + (zero_pair,)
+            for c in range(TILE // ROW_STEP):
+                carry = chunk(pl.multiple_of(OWN + t * TILE + c * ROW_STEP, 8), carry)
+            sums[pl.ds(first_sums + t, 1), :] = jnp.sum(own_total(carry[-1]), axis=0, keepdims=True)
+            return carry[:-1]
+
+        return lax.fori_loop(0, bands, band, run)
+
     shift16 = tall(shift, ROW_STEP)
     gram_phases = [(phase(gram_x.at[c], 8 + 2 * c, True), phase(gram_y.at[c], 9 + 2 * c, False)) for c in range(CYCLES)]
     finish += [p[2] for pair in gram_phases for p in pair]
@@ -502,15 +572,16 @@
             return jnp.broadcast_to(jnp.sum(picked, axis=1, keepdims=True), (8, LANES))
 
         def spread_band(dx, t, start, chunks):
-            own = tall(value_at(dx, t, 0), ROW_STEP)
-            side = tall(jnp.where(lane8 < LANES // 2, value_at(dx, t, 1), value_at(dx, t, -1)), ROW_STEP)
+            own, east, west = (value_at(dx, t, dy) for dy in (0, 1, -1))
+            side = jnp.where(lane8 < LANES // 2, west, east)
+            values = [tall(jnp.where(own_lanes(own, p), own, side), ROW_STEP) for p in range(panels)]
 
             def body(c, carry):
                 at = pl.ds(start + c * ROW_STEP, ROW_STEP)
                 for p in range(panels):
-                    value = ocean[p, at, :] * (side if p == edge else own)
-                    basis[KB, p, at, :] = value
-                    if dx == 0 and p < own_panels:
+                    value = ocean[p, at, :] * values[p]
+                    odd[p, at, :] = value
+                    if dx == 0:
                         inner = pl.ds(start - OWN + c * ROW_STEP, ROW_STEP)
                         sol[p, inner, :] = value if cycle == 0 else sol[p, inner, :] + value
                 return carry
@@ -523,65 +594,50 @@
         spread_band(1, 0, OWN + height, DEPTH // ROW_STEP)
 
         def first(r, carry):
-            out, values = stencil(KB, r)
+            out, values = stencil(odd, r)
             at = pl.ds(r, ROW_STEP)
             for p in range(panels):
                 v = res[p, at, :] - shift16 * (0.5 * out[p] + values[p])
+                even[p, at, :] = v
                 basis[0, p, at, :] = v
-                if p < own_panels and carry is not None:
+                if carry is not None:
                     square, total = carry
-                    carry = (square + fold(v * v), total + fold(v * ocean[p, at, :]))
+                    carry = (add_to(square, p, fold(v * v)), add_to(total, p, fold(v * ocean[p, at, :])))
             return carry
 
-        first(PAD, None)
-        first(OWN + height, None)
-        square = zero8
-        for t in range(bands):
-            square, total = lax.fori_loop(
-                0,
-                TILE // ROW_STEP,
-                lambda c, carry, t=t: first(OWN + t * TILE + c * ROW_STEP, carry),
-                (square, zero8),
-            )
-            sums[t : t + 1, :] = jnp.sum(total, axis=0, keepdims=True)
-        sums[64:65, :] = jnp.sum(square, axis=0, keepdims=True)
-
-        def step(j, carry):
-            previous = jnp.maximum(j - 2, 0)
+        (square,) = over_bands(first, 0, (zero_pair,))
+        sums[64:65, :] = jnp.sum(own_total(square), axis=0, keepdims=True)
+
+        def step(j, source, target):
             new_part = jnp.where(j == 1, 0.5, 1.0)
             old_part = jnp.where(j == 1, 0.0, 1.0)
 
             def chunk(r, carry):
-                out, values = stencil(j - 1, r)
+                out, values = stencil(source, r)
                 at = pl.ds(r, ROW_STEP)
                 for p in range(panels):
-                    v = new_part * out[p] - old_part * basis[previous, p, at, :]
+                    v = new_part * out[p] - old_part * target[p, at, :]
+                    target[p, at, :] = v
                     basis[j, p, at, :] = v
-                    if p < own_panels and carry is not None:
+                    if carry is not None:
                         square, cross, total = carry
                         carry = (
-                            square + fold(v * v),
-                            cross + fold(v * values[p]),
-                            total + fold(v * ocean[p, at, :]),
+                            add_to(square, p, fold(v * v)),
+                            add_to(cross, p, fold(v * values[p])),
+                            add_to(total, p, fold(v * ocean[p, at, :])),
                         )
                 return carry
 
-            chunk(PAD, None)
-            chunk(OWN + height, None)
-            square, cross = zero8, zero8
-            for t in range(bands):
-                square, cross, total = lax.fori_loop(
-                    0,
-                    TILE // ROW_STEP,
-                    lambda c, carry, t=t: chunk(OWN + t * TILE + c * ROW_STEP, carry),
-                    (square, cross, zero8),
-                )
-                sums[pl.ds(j * bands + t, 1), :] = jnp.sum(total, axis=0, keepdims=True)
-            sums[pl.ds(64 + j, 1), :] = jnp.sum(square, axis=0, keepdims=True)
-            sums[pl.ds(80 + j, 1), :] = jnp.sum(cross, axis=0, keepdims=True)
+            square, cross = over_bands(chunk, j * bands, (zero_pair, zero_pair))
+            sums[pl.ds(64 + j, 1), :] = jnp.sum(own_total(square), axis=0, keepdims=True)
+            sums[pl.ds(80 + j, 1), :] = jnp.sum(own_total(cross), axis=0, keepdims=True)
+
+        def two_steps(i, carry):
+            step(2 * i + 1, even, odd)
+            step(2 * i + 2, odd, even)
             return carry
 
-        lax.fori_loop(1, KB + 1, step, 0)
+        lax.fori_loop(0, KB // 2, two_steps, 0)
 
         row = lax.dot_general(
             jnp.ones((8, LANES), jnp.float32),
@@ -643,19 +699,12 @@
             answer = sol[p, rows, :]
             for j in range(KB):
                 answer = answer + w[j] * values[j]
-            if cycle < CYCLES - 1:
-                res[p, at, :] = residual
-                sol[p, rows, :] = answer
-            else:
-                columns = pl.ds(p * LANES, LANES)
-                residual_ref[rows, columns] = residual
-                solution_ref[rows, columns] = answer
+            res[p, at, :] = residual
+            sol[p, rows, :] = answer
 
         def update_own(c, carry):
-            for p in range(own_panels):
+            for p in range(panels):
                 update(OWN + c * ROW_STEP, p, c * ROW_STEP)
-            if cycle < CYCLES - 1:
-                update(OWN + c * ROW_STEP, edge, None)
             return carry
 
         lax.fori_loop(0, height // ROW_STEP, update_own, 0)
@@ -667,6 +716,27 @@
             coarse_y[cycle + 1, gy] = total_of(coarse_x.at[cycle + 1], size_x)
             starts_y[cycle + 1][0]()
 
+    def choose_back(c, carry):
+        for p in range(panels):
+            for q in range(own_panels):
+                goal, lane = place(16, LANES, q * LANES, True)
+                rows = pl.ds(p * LANES + c * 16, 16)
+                back[rows, q * LANES : (q + 1) * LANES] = jnp.where(
+                    goal == (lane + c * 16) * panels + p, 1.0, 0.0
+                ).astype(jnp.bfloat16)
+        return carry
+
+    lax.fori_loop(0, LANES // 16, choose_back, 0)
+
+    def unsettle(c, carry):
+        rows = pl.ds(c * block_rows, block_rows)
+        at = pl.ds(OWN + c * block_rows, block_rows)
+        solution_ref[rows, :] = placed(jnp.concatenate([sol[p, rows, :] for p in range(panels)], axis=1), back[...])
+        residual_ref[rows, :] = placed(jnp.concatenate([res[p, at, :] for p in range(panels)], axis=1), back[...])
+        return carry
+
+    lax.fori_loop(0, height // block_rows, unsettle, 0)
+
     for done in finish:
         done()
 
@@ -679,7 +749,7 @@
     bands = height // TILE
     f32 = jnp.float32
     field = pltpu.VMEM((panels, rows, LANES), f32)
-    block = pltpu.VMEM((own_panels, height, LANES), f32)
+    block = pltpu.VMEM((height, breadth), f32)
     any_spec = pl.BlockSpec(memory_space=pl.ANY)
     vmem = pl.BlockSpec(memory_space=pltpu.VMEM)
     smem = pl.BlockSpec(memory_space=pltpu.SMEM)
@@ -693,12 +763,18 @@
         scratch_shapes=[
             block,
             block,
-            pltpu.VMEM((own_panels, height, LANES), jnp.int32),
-            field,
-            field,
-            field,
-            block,
+            pltpu.VMEM((height, breadth), jnp.int32),
+            pltpu.VMEM((height, LANES), f32),
+            pltpu.VMEM((height, LANES), f32),
+            pltpu.VMEM((panels * LANES, panels * LANES), jnp.bfloat16),
+            pltpu.VMEM((panels * LANES, breadth), jnp.bfloat16),
+            field,
+            field,
+            field,
+            pltpu.VMEM((panels, height, LANES), f32),
             pltpu.VMEM((KB + 1, panels, rows, LANES), f32),
+            field,
+            field,
             field,
             field,
             field,
@@ -708,7 +784,7 @@
             pltpu.VMEM((2, height // GROUPS, LANES), f32),
             pltpu.VMEM((4, DEPTH, LANES), f32),
             pltpu.VMEM((4, DEPTH, LANES), f32),
-            pltpu.VMEM((2, 2, own_panels, DEPTH, LANES), f32),
+            pltpu.VMEM((2, 2, DEPTH, breadth), f32),
             tiles(bands),
             tiles(bands),
             pltpu.VMEM((LANES, LANES), f32),
@@ -721,14 +797,14 @@
             tiles(CYCLES, size_y),
             tiles(CYCLES, size_x),
             tiles(CYCLES, size_y),
-            dma((3 * own_panels,)),
+            dma((3,)),
             dma((10,)),
             dma((10,)),
             dma((12,)),
             dma((12,)),
         ],
         compiler_params=pltpu.CompilerParams(
-            collective_id=0, has_side_effects=True, vmem_limit_bytes=48 * 1024 * 1024
+            collective_id=0, has_side_effects=True, vmem_limit_bytes=60 * 1024 * 1024
         ),
     )(forcing, bathymetry, ocean_mask, aggregate_id, coarse_inverse, coarse_inverse)
 

time: 98.1 us -> 77.5 us (0.79)
  Pallas kernels: 91 us -> 73.9 us
  local copies, waits for them, and re-layouts: 6.08 us -> 2.72 us
    pallas_call x1, Pallas kernels: 91 us -> 73.9 us  [on_device(): pl.pallas_call(functools.partial(kernel, size_x, size_y), out_shape=(jax....]
    unnamed x12 -> x4, local copies, waits for them, and re-layouts: 6.08 us -> 2.72 us
where the time goes in v2:
time: 77.5 us; the launch traced here: 77.3 us
  Pallas kernels  73.9 us (95%)
  local copies, waits for them, and re-layouts  2.72 us (4%)
    pallas_call x1, Pallas kernels, on_device(): pl.pallas_call(functools.partial(kernel, size_x, size_y), out_shape=(jax....  73.9 us
    unnamed x4, local copies, waits for them, and re-layouts  2.72 us

profile of v2, /device:TPU:1, one launch (start us, length us, event | category | flops | bytes accessed | tf_op | source)
XLA Modules:
  0.0 77.3 jit_solution(12507038710260346481)
XLA Ops:
  0.6 73.9 %shard_map.68 = (f32[256,512]{1,0:T(8,128)}, f32[256,512]{1,0:T(8,128)}) custom-call(f32[256,512]{1,0:T(8,128)} %forcing_ref.1, f32[256,512]{1,0:T(8,128)} %depth_ref.1, s32[256,512]{1,0:T(8,128)} %mask_ref.1, s32[4,8]{1,0:T(4,128)} %agg_ref.1, f32[4,512]{1,0:T(4,128)} %inverse_smem.1, f32[4,512]{1,0:T(4,128)} %inverse_smem.1), custom_call_target="tpu_custom_call" | custom-call | tf_op jit(solution)/shard_map/pallas_call | solution.py:758
  74.5 0.0 copy-start
  74.5 1.9 %copy.9 = f32[256,512]{1,0:T(8,128)} copy(f32[256,512]{1,0:T(8,128)} %get-tuple-element.4) | data formatting | bytes 1048576
  76.5 0.0 copy-done
  76.5 0.8 %copy.10 = f32[256,512]{1,0:T(8,128)} copy(f32[256,512]{1,0:T(8,128)S(1)} %copy-done) | data formatting | bytes 1048576
Async XLA Ops:
  74.5 1.9 %copy-start = (f32[256,512]{1,0:T(8,128)S(1)}, f32[256,512]{1,0:T(8,128)}, u32[]{:S(2)}) copy-start(f32[256,512]{1,0:T(8,128)} %get-tuple-element.5) | copy-start | bytes 1572868

commit v3 on v2

--- a/solution.py
+++ b/solution.py
@@ -55,6 +55,18 @@
     return jnp.dot(high, chooser, preferred_element_type=jnp.float32) + jnp.dot(
         low, chooser, preferred_element_type=jnp.float32
     )
+
+
+def exact_placed(chooser, x):
+    high, rest = split(x)
+    low = (x - high.astype(jnp.float32) - rest.astype(jnp.float32)).astype(jnp.bfloat16)
+    return sum(jnp.dot(chooser, part, preferred_element_type=jnp.float32) for part in (high, rest, low))
+
+
+def exact_moved(x, chooser):
+    high, rest = split(x)
+    low = (x - high.astype(jnp.float32) - rest.astype(jnp.float32)).astype(jnp.bfloat16)
+    return sum(jnp.dot(part, chooser, preferred_element_type=jnp.float32) for part in (high, rest, low))
 
 
 def small_solve(vv, vp):
@@ -133,16 +145,15 @@
     mask_ref,
     agg_ref,
     inverse_ref,
-    inverse_smem,
     solution_ref,
     residual_ref,
+    back,
     in_f,
     in_b,
     in_m,
     side_w,
     side_r,
     chooser,
-    back,
     wet,
     ocean,
     res,
@@ -161,7 +172,10 @@
     got_corner,
     got_row,
     inverse_rows,
-    perm_rows,
+    selector,
+    permuted,
+    bulk_x,
+    bulk_y,
     sums,
     factors,
     first_x,
@@ -189,7 +203,9 @@
     first_row = (gx * size_y + gy) * bands
 
     loads = []
-    for index, (source, target) in enumerate(((depth_ref, in_b), (mask_ref, in_m), (forcing_ref, in_f))):
+    for index, (source, target) in enumerate(
+        ((depth_ref, in_b), (mask_ref, in_m), (forcing_ref, in_f), (inverse_ref, bulk_x.at[gx]))
+    ):
         copy = pltpu.make_async_copy(source, target, in_sem.at[index])
         copy.start()
         loads.append(copy)
@@ -222,12 +238,6 @@
             for array in (wet, even, odd):
                 array[p, start : start + PAD, :] = zero8
     sums[...] = jnp.zeros_like(sums)
-    inverse_rows[...] = jnp.zeros_like(inverse_rows)
-    for s in range(bands):
-        for c in range(-(-n_agg // LANES)):
-            width = min(LANES, n_agg - c * LANES)
-            inverse_rows[s, c : c + 1, 0:width] = inverse_ref[s : s + 1, c * LANES : c * LANES + width]
-
     def place(rows, columns, column_base, transposed):
         line = lax.broadcasted_iota(jnp.int32, (rows, columns), 1 if transposed else 0) + column_base
         spot = lax.broadcasted_iota(jnp.int32, (rows, columns), 0 if transposed else 1)
@@ -246,6 +256,11 @@
 
     for copy in loads:
         copy.wait()
+    inverse_rows[...] = jnp.zeros_like(inverse_rows)
+    for s in range(bands):
+        for c in range(-(-n_agg // LANES)):
+            width = min(LANES, n_agg - c * LANES)
+            inverse_rows[s, c : c + 1, 0:width] = bulk_x[gx, s : s + 1, c * LANES : c * LANES + width]
 
     band_sums = []
     for t in range(bands):
@@ -363,6 +378,10 @@
     start_my, wait_my, done_my = phase(max_y, 3, False)
     finish += [done_fx, done_fy, done_mx, done_my]
     start_fx()
+    start_bx, wait_bx, done_bx = phase(bulk_x, 12, True)
+    start_by, wait_by, done_by = phase(bulk_y, 13, False)
+    finish += [done_bx, done_by]
+    start_bx()
 
     own_rows = pl.ds(0, breadth)
     block_rows = 64
@@ -484,7 +503,8 @@
 
     wait_fy()
     rhs = total_of(first_y, size_y, 0)
-    table = total_of(first_y, size_y, 1).astype(jnp.int32) - 1
+    labels = total_of(first_y, size_y, 1)
+    table = labels.astype(jnp.int32) - 1
 
     def spread_coarse(rhs, rows, buffer):
         tile = zero8
@@ -492,27 +512,24 @@
             tile = jnp.where(table == first_row + s, splat_sum(rows[s] * rhs), tile)
         buffer[gx] = tile
 
-    spread_coarse(rhs, inverse_rows, coarse_x.at[0])
-    starts = [phase(coarse_x.at[c], 4 + 2 * c, True) for c in range(CYCLES)]
-    starts_y = [phase(coarse_y.at[c], 5 + 2 * c, False) for c in range(CYCLES)]
-    finish += [s[2] for s in starts] + [s[2] for s in starts_y]
-    starts[0][0]()
+    spread_coarse(rhs, inverse_rows, coarse_x)
+    start_cx, wait_cx, done_cx = phase(coarse_x, 4, True)
+    start_cy, wait_cy, done_cy = phase(coarse_y, 5, False)
+    finish += [done_cx, done_cy]
+    start_cx()
 
     wait_mx()
     max_y[gy] = functools.reduce(jnp.maximum, [max_x[i] for i in range(size_x)])
     start_my()
 
-    def permute(q, carry):
-        match = table == q
-        return tuple(jnp.where(match, inverse_smem[s, q], carry[s]) for s in range(bands))
-
-    permuted = lax.fori_loop(0, n_agg, permute, (zero8,) * bands, unroll=8)
-    for s in range(bands):
-        perm_rows[s] = permuted[s]
-
-    starts[0][1]()
-    coarse_y[0, gy] = total_of(coarse_x.at[0], size_x)
-    starts_y[0][0]()
+    wait_cx()
+    coarse_y[gy] = total_of(coarse_x, size_x)
+    start_cy()
+
+    wait_bx()
+    for i in range(size_x):
+        bulk_y[gy, i * bands : (i + 1) * bands, :] = bulk_x[i]
+
     wait_my()
     largest = functools.reduce(jnp.maximum, [max_y[i] for i in range(size_y)])
     for move in (4, 2, 1):
@@ -562,17 +579,62 @@
     gram_phases = [(phase(gram_x.at[c], 8 + 2 * c, True), phase(gram_y.at[c], 9 + 2 * c, False)) for c in range(CYCLES)]
     finish += [p[2] for pair in gram_phases for p in pair]
 
+    strips = [(-1, bands - 1)] + [(0, t) for t in range(bands)] + [(1, 0)]
+
+    def around(tile):
+        rows_of = {dx: sub_total(jnp.where(sub == gx + dx, tile, 0.0)) for dx in (-1, 0, 1)}
+        found = []
+        for dx, t in strips:
+            for dy in (-1, 0, 1):
+                picked = jnp.where(lane8 == (gy + dy) * bands + t, rows_of[dx], 0.0)
+                found.append(jnp.broadcast_to(jnp.sum(picked, axis=1, keepdims=True), (8, LANES)))
+        return found
+
+    def choose_rows():
+        slot = lax.broadcasted_iota(jnp.int32, (1, n_agg), 1)
+        in_slot = lax.rem(slot, size_x * bands)
+        row = (lax.div(in_slot, bands) * size_y + lax.div(slot, size_x * bands)) * bands + lax.rem(in_slot, bands)
+        selector[...] = jnp.zeros_like(selector)
+        for k, label in enumerate(around(labels)):
+            wide = jnp.concatenate([label[0:1]] * max(1, n_agg // LANES), axis=1)[:, 0:n_agg]
+            selector[k : k + 1, :] = jnp.where((row + 1).astype(jnp.float32) == wide, 1.0, 0.0)
+
+    def permute_rows():
+        chunks = max(1, n_agg // LANES)
+        width, per = n_agg // chunks, size_y // chunks
+        rows = None
+        for c in range(chunks):
+            part = exact_placed(
+                selector[:, c * width : (c + 1) * width].astype(jnp.bfloat16),
+                jnp.concatenate([bulk_y[c * per + i] for i in range(per)], axis=0),
+            )
+            rows = part if rows is None else rows + part
+        column = lax.broadcasted_iota(jnp.int32, (n_agg, LANES), 0)
+        for i in range(size_x):
+            unit = jnp.where(column == table[i : i + 1, :], 1.0, 0.0).astype(jnp.bfloat16)
+            permuted[i] = exact_moved(rows, unit)
+
+    def choose_back(c, carry):
+        for p in range(panels):
+            for q in range(own_panels):
+                goal, lane = place(16, LANES, q * LANES, True)
+                rows = pl.ds(p * LANES + c * 16, 16)
+                back[rows, q * LANES : (q + 1) * LANES] = jnp.where(
+                    goal == (lane + c * 16) * panels + p, 1.0, 0.0
+                ).astype(jnp.bfloat16)
+        return carry
+
+    next_values = None
     for cycle in range(CYCLES):
-        starts_y[cycle][1]()
-        tile = total_of(coarse_y.at[cycle], size_y)
-        rows_of = {dx: sub_total(jnp.where(sub == gx + dx, tile, 0.0)) for dx in (-1, 0, 1)}
-
-        def value_at(dx, t, dy):
-            picked = jnp.where(lane8 == (gy + dy) * bands + t, rows_of[dx], 0.0)
-            return jnp.broadcast_to(jnp.sum(picked, axis=1, keepdims=True), (8, LANES))
-
-        def spread_band(dx, t, start, chunks):
-            own, east, west = (value_at(dx, t, dy) for dy in (0, 1, -1))
+        if cycle == 0:
+            wait_cy()
+            values_at = around(total_of(coarse_y, size_y))
+        else:
+            values_at = next_values
+
+        def spread_band(strip, start, chunks):
+            west, own, east = values_at[3 * strip : 3 * strip + 3]
+            dx = strips[strip][0]
             side = jnp.where(lane8 < LANES // 2, west, east)
             values = [tall(jnp.where(own_lanes(own, p), own, side), ROW_STEP) for p in range(panels)]
 
@@ -588,10 +650,12 @@
 
             lax.fori_loop(0, chunks, body, 0)
 
-        spread_band(-1, bands - 1, PAD, DEPTH // ROW_STEP)
+        spread_band(0, PAD, DEPTH // ROW_STEP)
         for t in range(bands):
-            spread_band(0, t, OWN + t * TILE, TILE // ROW_STEP)
-        spread_band(1, 0, OWN + height, DEPTH // ROW_STEP)
+            spread_band(1 + t, OWN + t * TILE, TILE // ROW_STEP)
+        spread_band(1 + bands, OWN + height, DEPTH // ROW_STEP)
+        if cycle == 0:
+            start_by()
 
         def first(r, carry):
             out, values = stencil(odd, r)
@@ -649,9 +713,16 @@
         (start_gx, wait_gx, _), (start_gy, wait_gy, _) = gram_phases[cycle]
         gram_x[cycle, gx] = jnp.where(sub == gx, row, 0.0)
         start_gx()
+        if cycle == 0:
+            choose_rows()
+        else:
+            lax.fori_loop(0, LANES // 16, choose_back, 0)
         wait_gx()
         gram_y[cycle, gy] = total_of(gram_x.at[cycle], size_x)
         start_gy()
+        if cycle == 0:
+            wait_by()
+            permute_rows()
         wait_gy()
         gathered = [gram_y[cycle, i] for i in range(size_y)]
         whole = sub_total(functools.reduce(jnp.add, gathered))
@@ -680,8 +751,11 @@
                     part = part + pltpu.roll(part, move, 1)
                     move *= 2
                 rhs = jnp.where(group == i, part, rhs)
-            spread_coarse(rhs, perm_rows, coarse_x.at[cycle + 1])
-            starts[cycle + 1][0]()
+            found = permuted[0] * rhs[0:1, :]
+            for i in range(1, size_x):
+                found = found + permuted[i] * rhs[i : i + 1, :]
+            found = jnp.broadcast_to(jnp.sum(found, axis=1, keepdims=True), found.shape)
+            next_values = [jnp.broadcast_to(found[k : k + 1, :], (8, LANES)) for k in range(3 * len(strips))]
 
         w = [tall(factors[j], ROW_STEP) for j in range(KB)]
         c_all = [tall(factors[KB + a], ROW_STEP) for a in range(KB + 1)]
@@ -699,8 +773,12 @@
             answer = sol[p, rows, :]
             for j in range(KB):
                 answer = answer + w[j] * values[j]
-            res[p, at, :] = residual
-            sol[p, rows, :] = answer
+            if cycle < CYCLES - 1:
+                res[p, at, :] = residual
+                sol[p, rows, :] = answer
+            else:
+                residual_ref[p, rows, :] = residual
+                solution_ref[p, rows, :] = answer
 
         def update_own(c, carry):
             for p in range(panels):
@@ -712,33 +790,24 @@
             for p in range(panels):
                 update(PAD, p, None)
                 update(OWN + height, p, None)
-            starts[cycle + 1][1]()
-            coarse_y[cycle + 1, gy] = total_of(coarse_x.at[cycle + 1], size_x)
-            starts_y[cycle + 1][0]()
-
-    def choose_back(c, carry):
-        for p in range(panels):
-            for q in range(own_panels):
-                goal, lane = place(16, LANES, q * LANES, True)
-                rows = pl.ds(p * LANES + c * 16, 16)
-                back[rows, q * LANES : (q + 1) * LANES] = jnp.where(
-                    goal == (lane + c * 16) * panels + p, 1.0, 0.0
-                ).astype(jnp.bfloat16)
-        return carry
-
-    lax.fori_loop(0, LANES // 16, choose_back, 0)
-
-    def unsettle(c, carry):
-        rows = pl.ds(c * block_rows, block_rows)
-        at = pl.ds(OWN + c * block_rows, block_rows)
-        solution_ref[rows, :] = placed(jnp.concatenate([sol[p, rows, :] for p in range(panels)], axis=1), back[...])
-        residual_ref[rows, :] = placed(jnp.concatenate([res[p, at, :] for p in range(panels)], axis=1), back[...])
-        return carry
-
-    lax.fori_loop(0, height // block_rows, unsettle, 0)
 
     for done in finish:
         done()
+
+
+def to_natural(solution_ref, residual_ref, back, solution_out, residual_out, parts, sems):
+    panels, height = solution_ref.shape[:2]
+    rows = parts.shape[1]
+    copies = []
+    for index in range(height // rows):
+        at = pl.ds(index * rows, rows)
+        for which, (source, target) in enumerate(((solution_ref, solution_out), (residual_ref, residual_out))):
+            slot = 2 * index + which
+            parts[slot] = placed(jnp.concatenate([source[p, at, :] for p in range(panels)], axis=1), back[...])
+            copies.append(pltpu.make_async_copy(parts.at[slot], target.at[at, :], sems.at[slot]))
+            copies[-1].start()
+    for copy in copies:
+        copy.wait()
 
 
 def on_device(size_x, size_y, forcing, bathymetry, ocean_mask, aggregate_id, coarse_inverse):
@@ -750,16 +819,24 @@
     f32 = jnp.float32
     field = pltpu.VMEM((panels, rows, LANES), f32)
     block = pltpu.VMEM((height, breadth), f32)
-    any_spec = pl.BlockSpec(memory_space=pl.ANY)
+    any_spec = pl.BlockSpec(memory_space=pltpu.MemorySpace.HBM)
     vmem = pl.BlockSpec(memory_space=pltpu.VMEM)
     smem = pl.BlockSpec(memory_space=pltpu.SMEM)
     tiles = lambda *lead: pltpu.VMEM(lead + (8, LANES), f32)
     dma = pltpu.SemaphoreType.DMA
-    return pl.pallas_call(
+    n_agg = coarse_inverse.shape[1]
+    wanted = -(-3 * (bands + 2) // 8) * 8
+    dealt = jax.ShapeDtypeStruct((panels, height, LANES), f32)
+    back = jax.ShapeDtypeStruct((panels * LANES, breadth), jnp.bfloat16)
+    forcing, bathymetry, ocean_mask, aggregate_id, coarse_inverse = (
+        pltpu.with_memory_space_constraint(x, pltpu.MemorySpace.HBM)
+        for x in (forcing, bathymetry, ocean_mask, aggregate_id, coarse_inverse)
+    )
+    answer, residual, back = pl.pallas_call(
         functools.partial(kernel, size_x, size_y),
-        out_shape=(jax.ShapeDtypeStruct((height, breadth), f32),) * 2,
-        in_specs=[any_spec, any_spec, any_spec, smem, vmem, smem],
-        out_specs=(vmem, vmem),
+        out_shape=(dealt, dealt, back),
+        in_specs=[any_spec, any_spec, any_spec, smem, any_spec],
+        out_specs=(vmem, vmem, vmem),
         scratch_shapes=[
             block,
             block,
@@ -767,7 +844,6 @@
             pltpu.VMEM((height, LANES), f32),
             pltpu.VMEM((height, LANES), f32),
             pltpu.VMEM((panels * LANES, panels * LANES), jnp.bfloat16),
-            pltpu.VMEM((panels * LANES, breadth), jnp.bfloat16),
             field,
             field,
             field,
@@ -786,27 +862,40 @@
             pltpu.VMEM((4, DEPTH, LANES), f32),
             pltpu.VMEM((2, 2, DEPTH, breadth), f32),
             tiles(bands),
-            tiles(bands),
+            pltpu.VMEM((wanted, n_agg), f32),
+            pltpu.VMEM((size_x, wanted, LANES), f32),
+            pltpu.VMEM((size_x, bands, n_agg), f32),
+            pltpu.VMEM((size_y, size_x * bands, n_agg), f32),
             pltpu.VMEM((LANES, LANES), f32),
             tiles(2 * KB + 1),
             tiles(size_x, 2),
             tiles(size_y, 2),
             tiles(size_x),
             tiles(size_y),
+            tiles(size_x),
+            tiles(size_y),
             tiles(CYCLES, size_x),
             tiles(CYCLES, size_y),
-            tiles(CYCLES, size_x),
-            tiles(CYCLES, size_y),
-            dma((3,)),
+            dma((4,)),
             dma((10,)),
             dma((10,)),
-            dma((12,)),
-            dma((12,)),
+            dma((14,)),
+            dma((14,)),
         ],
         compiler_params=pltpu.CompilerParams(
-            collective_id=0, has_side_effects=True, vmem_limit_bytes=60 * 1024 * 1024
+            collective_id=0, has_side_effects=True, vmem_limit_bytes=40 * 1024 * 1024
         ),
-    )(forcing, bathymetry, ocean_mask, aggregate_id, coarse_inverse, coarse_inverse)
+    )(forcing, bathymetry, ocean_mask, aggregate_id, coarse_inverse)
+    part = 64
+    count = 2 * (height // part)
+    return pl.pallas_call(
+        to_natural,
+        out_shape=(jax.ShapeDtypeStruct((height, breadth), f32),) * 2,
+        in_specs=[vmem, vmem, vmem],
+        out_specs=(any_spec, any_spec),
+        scratch_shapes=[pltpu.VMEM((count, part, breadth), f32), dma((count,))],
+        compiler_params=pltpu.CompilerParams(vmem_limit_bytes=16 * 1024 * 1024),
+    )(answer, residual, back)
 
 
 def solution(mesh):

time: 77.5 us -> 66.4 us (0.86)
  Pallas kernels: 73.9 us -> 65.6 us
  local copies, waits for them, and re-layouts: 2.72 us -> 0 us
    pallas_call x1 -> x2, Pallas kernels: 73.9 us -> 65.6 us  [the longest x1 62.9 us: on_device(): pl.pallas_call(functools.partial(kernel, size_x, size_y), out_shape=(deal...]
    unnamed x4 -> x0, local copies, waits for them, and re-layouts: 2.72 us -> none
where the time goes in v3:
time: 66.4 us; the launch traced here: 66.2 us
  Pallas kernels  65.6 us (99%)
    pallas_call x1, Pallas kernels, on_device(): pl.pallas_call(functools.partial(kernel, size_x, size_y), out_shape=(deal...  62.9 us
    pallas_call x1, Pallas kernels, on_device(): pl.pallas_call(to_natural, out_shape=(jax.ShapeDtypeStruct((height, bread...  2.69 us

profile of v3, /device:TPU:1, one launch (start us, length us, event | category | flops | bytes accessed | tf_op | source)
XLA Modules:
  0.0 66.2 jit_solution(2643674057630752613)
XLA Ops:
  0.6 62.9 %shard_map.68 = (f32[5,256,128]{2,1,0:T(8,128)S(1)}, f32[5,256,128]{2,1,0:T(8,128)S(1)}, bf16[640,512]{1,0:T(8,128)(2,1)S(1)}) custom-call(f32[256,512]{1,0:T(8,128)} %forcing_ref.1, f32[256,512]{1,0:T(8,128)} %depth_ref.1, s32[256,512]{1,0:T(8,128)} %mask_ref.1, s32[4,8]{1,0:T(4,128)} %agg_ref.1, f32[4,512]{1,0:T(4,128)} %inverse_ref.1), custom_call_target="tpu_custom_call" | custom-call | tf_op jit(solution)/shard_map/pallas_call | solution.py:835
  63.5 2.7 %shard_map.69 = (f32[256,512]{1,0:T(8,128)}, f32[256,512]{1,0:T(8,128)}) custom-call(f32[5,256,128]{2,1,0:T(8,128)S(1)} %get-tuple-element.5.solution_ref, f32[5,256,128]{2,1,0:T(8,128)S(1)} %get-tuple-element.6.residual_ref, bf16[640,512]{1,0:T(8,128)(2,1)S(1)} %get-tuple-element.7.back), custom_call_target="tpu_custom_call" | custom-call | tf_op jit(solution)/shard_map/pallas_call | solution.py:891

commit v4 on v3

--- a/solution.py
+++ b/solution.py
@@ -173,19 +173,15 @@
     got_row,
     inverse_rows,
     selector,
-    permuted,
+    chosen,
     bulk_x,
     bulk_y,
     sums,
     factors,
-    first_x,
-    first_y,
-    max_x,
-    max_y,
-    coarse_x,
-    coarse_y,
-    gram_x,
-    gram_y,
+    first_all,
+    max_all,
+    coarse_all,
+    gram_all,
     in_sem,
     halo_send,
     halo_recv,
@@ -200,7 +196,6 @@
     rows_all = wet.shape[1]
     group_rows = height // GROUPS
     gx, gy = lax.axis_index("gx"), lax.axis_index("gy")
-    first_row = (gx * size_y + gy) * bands
 
     loads = []
     for index, (source, target) in enumerate(
@@ -221,12 +216,23 @@
         dx, dy = SIDES[side]
         return (lax.rem(gx + dx + size_x, size_x), lax.rem(gy + dy + size_y, size_y))
 
-    for d in range(1, size_x):
-        pl.semaphore_signal(barrier, inc=1, device_id=peer_x(d), device_id_type=MESH)
-    for d in range(1, size_y):
-        pl.semaphore_signal(barrier, inc=1, device_id=peer_y(d), device_id_type=MESH)
-    for side in (NW, NE, SW, SE):
-        pl.semaphore_signal(barrier, inc=1, device_id=neighbour(side), device_id_type=MESH)
+    others = size_x * size_y - 1
+
+    xs = [lax.rem(gx + d, size_x) for d in range(size_x)]
+    ys = [lax.rem(gy + d, size_y) for d in range(size_y)]
+
+    def hops(d):
+        ring = lambda k: min(k, 4 - k)
+        dx, dy = divmod(d, size_y)
+        return ring(dx // 2) + ring(dy % 4) + ring(dy // 4)
+
+    far_first = sorted(range(1, others + 1), key=lambda d: -hops(d))
+
+    def peer(d):
+        return (xs[d // size_y], ys[d % size_y])
+
+    for d in far_first:
+        pl.semaphore_signal(barrier, inc=1, device_id=peer(d), device_id_type=MESH)
 
     sub = lax.broadcasted_iota(jnp.int32, (8, LANES), 0)
     lane8 = lax.broadcasted_iota(jnp.int32, (8, LANES), 1)
@@ -257,10 +263,8 @@
     for copy in loads:
         copy.wait()
     inverse_rows[...] = jnp.zeros_like(inverse_rows)
-    for s in range(bands):
-        for c in range(-(-n_agg // LANES)):
-            width = min(LANES, n_agg - c * LANES)
-            inverse_rows[s, c : c + 1, 0:width] = bulk_x[gx, s : s + 1, c * LANES : c * LANES + width]
+    chosen[...] = jnp.zeros_like(chosen)
+    inverse_rows[0:bands, 0:n_agg] = bulk_x[gx]
 
     band_sums = []
     for t in range(bands):
@@ -330,8 +334,12 @@
     def phase(buffer, index, along_x):
         size, me, peer = (size_x, gx, peer_x) if along_x else (size_y, gy, peer_y)
 
+        def far(d):
+            ring = lambda k: -min(k, 4 - k)
+            return ring(d // 2) if along_x else ring(d % 4) + ring(d // 4)
+
         def start():
-            for d in range(1, size):
+            for d in sorted(range(1, size), key=far):
                 pltpu.make_async_remote_copy(
                     src_ref=buffer.at[me],
                     dst_ref=buffer.at[me],
@@ -354,32 +362,72 @@
 
         return start, (lambda: whole().wait_recv()), (lambda: whole().wait_send())
 
-    def total_of(buffer, size, *index):
-        return functools.reduce(jnp.add, [buffer[(i,) + index] for i in range(size)])
+    me = gx * size_y + gy
+
+    def direct(buffer, index):
+        def start(row):
+            buffer[pl.ds(me, 1), :] = row
+            mine = buffer.at[pl.ds(me, 1), :]
+
+            for d in far_first:
+                pltpu.make_async_remote_copy(
+                    src_ref=mine,
+                    dst_ref=mine,
+                    send_sem=phase_send.at[index],
+                    recv_sem=phase_recv.at[index],
+                    device_id=peer(d),
+                    device_id_type=MESH,
+                ).start()
+
+        def whole():
+            part = buffer.at[pl.ds(0, others), :]
+            return pltpu.make_async_remote_copy(
+                src_ref=part,
+                dst_ref=part,
+                send_sem=phase_send.at[index],
+                recv_sem=phase_recv.at[index],
+                device_id=peer(1),
+                device_id_type=MESH,
+            )
+
+        return start, (lambda: whole().wait_recv()), (lambda: whole().wait_send())
+
+    groups = -(-(others + 1) // 8)
+
+    def rows_of(buffer, i):
+        return buffer[8 * i : 8 * i + 8, :]
+
+    def by_label(values):
+        total = [zero8] * pieces
+        for i in range(groups):
+            table = rows_of(first_all, i)
+            for t in range(bands):
+                label = jnp.broadcast_to(table[:, bands + t : bands + t + 1], (8, LANES))
+                value = jnp.broadcast_to(values[i][:, t : t + 1], (8, LANES))
+                for c in range(pieces):
+                    total[c] = total[c] + jnp.where(label == numbers[c], value, 0.0)
+        return jnp.concatenate([jnp.sum(x, axis=0, keepdims=True) for x in total], axis=1)
 
     finish = []
 
-    aggregate = sub * LANES + lane8
-    by_aggregate, where_table = zero8, zero8
+    pieces = -(-n_agg // LANES)
+    numbers = [(lane8 + (c * LANES + 1)).astype(jnp.float32) for c in range(pieces)]
+    first_row_values = zero8
     for t in range(bands):
-        label = agg_ref[t, 0]
-        by_aggregate = jnp.where(aggregate == label, band_sums[t], by_aggregate)
-        here = (sub == gx) & (lane8 == gy * bands + t)
-        where_table = jnp.where(here, (label + 1).astype(jnp.float32), where_table)
-    first_x[gx, 0] = by_aggregate
-    first_x[gx, 1] = where_table
-
-    pl.semaphore_wait(barrier, size_x + size_y - 2 + 4)
+        first_row_values = jnp.where(lane8 == t, band_sums[t], first_row_values)
+        label = (agg_ref[t, 0] + 1).astype(jnp.float32)
+        first_row_values = jnp.where(lane8 == bands + t, label, first_row_values)
+
+    pl.semaphore_wait(barrier, others)
     for copy in halos:
         copy.start()
-    start_fx, wait_fx, done_fx = phase(first_x, 0, True)
-    start_fy, wait_fy, done_fy = phase(first_y, 1, False)
-    start_mx, wait_mx, done_mx = phase(max_x, 2, True)
-    start_my, wait_my, done_my = phase(max_y, 3, False)
-    finish += [done_fx, done_fy, done_mx, done_my]
-    start_fx()
-    start_bx, wait_bx, done_bx = phase(bulk_x, 12, True)
-    start_by, wait_by, done_by = phase(bulk_y, 13, False)
+    start_f, wait_f, done_f = direct(first_all, 0)
+    start_m, wait_m, done_m = direct(max_all, 1)
+    start_c, wait_c, done_c = direct(coarse_all, 2)
+    finish += [done_f, done_m, done_c]
+    start_f(first_row_values[0:1])
+    start_bx, wait_bx, done_bx = phase(bulk_x, 5, True)
+    start_by, wait_by, done_by = phase(bulk_y, 6, False)
     finish += [done_bx, done_by]
     start_bx()
 
@@ -395,11 +443,6 @@
         return carry
 
     lax.fori_loop(0, height // block_rows, settle, 0)
-
-    wait_fx()
-    for part in range(2):
-        first_y[gy, part] = total_of(first_x, size_x, part)
-    start_fy()
 
     for copy in halos:
         copy.wait()
@@ -468,6 +511,9 @@
         return tuple(total + x if i == kind(p) else total for i, total in enumerate(pair))
 
     zero_pair = (zero8, zero8)
+
+    def row_at(i):
+        return pl.ds(i, 1)
 
     def faces(r, top):
         values = [wet[p, pl.ds(r, ROW_STEP), :] for p in range(panels)]
@@ -494,44 +540,38 @@
     top = lax.fori_loop(
         0, height // ROW_STEP, lambda c, top: faces(OWN + c * ROW_STEP, top), (jnp.ones((8, LANES), jnp.float32),) * 2
     )
-    max_x[gx] = jnp.maximum(
+    top = jnp.maximum(
         jnp.where(own_lanes(top[0], 0), top[0], 1.0), jnp.where(own_lanes(top[1], panels - 1), top[1], 1.0)
     )
-    start_mx()
+    start_m(jnp.max(top, axis=0, keepdims=True))
     faces(PAD, None)
     faces(OWN + height, None)
 
-    wait_fy()
-    rhs = total_of(first_y, size_y, 0)
-    labels = total_of(first_y, size_y, 1)
-    table = labels.astype(jnp.int32) - 1
-
-    def spread_coarse(rhs, rows, buffer):
-        tile = zero8
-        for s in range(bands):
-            tile = jnp.where(table == first_row + s, splat_sum(rows[s] * rhs), tile)
-        buffer[gx] = tile
-
-    spread_coarse(rhs, inverse_rows, coarse_x)
-    start_cx, wait_cx, done_cx = phase(coarse_x, 4, True)
-    start_cy, wait_cy, done_cy = phase(coarse_y, 5, False)
-    finish += [done_cx, done_cy]
-    start_cx()
-
-    wait_mx()
-    max_y[gy] = functools.reduce(jnp.maximum, [max_x[i] for i in range(size_x)])
-    start_my()
-
-    wait_cx()
-    coarse_y[gy] = total_of(coarse_x, size_x)
-    start_cy()
+    wait_f()
+    rhs = by_label([rows_of(first_all, i) for i in range(groups)])
+    coarse_row = jnp.zeros((1, LANES), jnp.float32)
+    lane1 = lax.broadcasted_iota(jnp.int32, (1, LANES), 1)
+    for s in range(bands):
+        product = jnp.sum(inverse_rows[s : s + 1, :] * rhs, axis=1, keepdims=True)
+        coarse_row = jnp.where(lax.rem(lane1, bands) == s, product, coarse_row)
+    start_c(coarse_row)
+
+    strips = [(-1, bands - 1)] + [(0, t) for t in range(bands)] + [(1, 0)]
+    labels = []
+    for dx, t in strips:
+        for dy in (-1, 0, 1):
+            inside = (gx + dx >= 0) & (gx + dx < size_x) & (gy + dy >= 0) & (gy + dy < size_y)
+            device = jnp.where(inside, me + dx * size_y + dy, me)
+            label = first_all[pl.ds(device, 1), :][:, bands + t : bands + t + 1]
+            label = jnp.broadcast_to(label, (1, LANES))
+            labels.append(jnp.where(inside, label, 0.0))
 
     wait_bx()
     for i in range(size_x):
         bulk_y[gy, i * bands : (i + 1) * bands, :] = bulk_x[i]
 
-    wait_my()
-    largest = functools.reduce(jnp.maximum, [max_y[i] for i in range(size_y)])
+    wait_m()
+    largest = functools.reduce(jnp.maximum, [rows_of(max_all, i) for i in range(groups)])
     for move in (4, 2, 1):
         largest = jnp.maximum(largest, pltpu.roll(largest, move, 0))
     shift = jnp.broadcast_to(jnp.max(largest, axis=1, keepdims=True), (8, LANES))
@@ -576,18 +616,22 @@
         return lax.fori_loop(0, bands, band, run)
 
     shift16 = tall(shift, ROW_STEP)
-    gram_phases = [(phase(gram_x.at[c], 8 + 2 * c, True), phase(gram_y.at[c], 9 + 2 * c, False)) for c in range(CYCLES)]
-    finish += [p[2] for pair in gram_phases for p in pair]
-
-    strips = [(-1, bands - 1)] + [(0, t) for t in range(bands)] + [(1, 0)]
-
-    def around(tile):
-        rows_of = {dx: sub_total(jnp.where(sub == gx + dx, tile, 0.0)) for dx in (-1, 0, 1)}
+    grams = [direct(gram_all.at[c], 3 + c) for c in range(CYCLES)]
+    finish += [p[2] for p in grams]
+
+    def coarse_values():
+        row = jnp.zeros((1, LANES), jnp.float32)
+        for k, label in enumerate(labels):
+            row = jnp.where(lax.div(lane1, bands) == k, label, row)
+        total = zero8
+        for i in range(groups):
+            number = ((8 * i + sub) * bands + lax.rem(lane8, bands) + 1).astype(jnp.float32)
+            total = total + jnp.where(number == row, rows_of(coarse_all, i), 0.0)
+        total = sub_total(total)
         found = []
-        for dx, t in strips:
-            for dy in (-1, 0, 1):
-                picked = jnp.where(lane8 == (gy + dy) * bands + t, rows_of[dx], 0.0)
-                found.append(jnp.broadcast_to(jnp.sum(picked, axis=1, keepdims=True), (8, LANES)))
+        for k in range(len(labels)):
+            picked = jnp.where(lax.div(lane8, bands) == k, total, 0.0)
+            found.append(jnp.broadcast_to(jnp.sum(picked, axis=1, keepdims=True), (8, LANES)))
         return found
 
     def choose_rows():
@@ -595,8 +639,8 @@
         in_slot = lax.rem(slot, size_x * bands)
         row = (lax.div(in_slot, bands) * size_y + lax.div(slot, size_x * bands)) * bands + lax.rem(in_slot, bands)
         selector[...] = jnp.zeros_like(selector)
-        for k, label in enumerate(around(labels)):
-            wide = jnp.concatenate([label[0:1]] * max(1, n_agg // LANES), axis=1)[:, 0:n_agg]
+        for k, label in enumerate(labels):
+            wide = jnp.concatenate([label] * pieces, axis=1)[:, 0:n_agg]
             selector[k : k + 1, :] = jnp.where((row + 1).astype(jnp.float32) == wide, 1.0, 0.0)
 
     def permute_rows():
@@ -609,10 +653,7 @@
                 jnp.concatenate([bulk_y[c * per + i] for i in range(per)], axis=0),
             )
             rows = part if rows is None else rows + part
-        column = lax.broadcasted_iota(jnp.int32, (n_agg, LANES), 0)
-        for i in range(size_x):
-            unit = jnp.where(column == table[i : i + 1, :], 1.0, 0.0).astype(jnp.bfloat16)
-            permuted[i] = exact_moved(rows, unit)
+        chosen[:, 0:n_agg] = rows
 
     def choose_back(c, carry):
         for p in range(panels):
@@ -627,8 +668,8 @@
     next_values = None
     for cycle in range(CYCLES):
         if cycle == 0:
-            wait_cy()
-            values_at = around(total_of(coarse_y, size_y))
+            wait_c()
+            values_at = coarse_values()
         else:
             values_at = next_values
 
@@ -657,6 +698,8 @@
         if cycle == 0:
             start_by()
 
+        with_totals = cycle < CYCLES - 1
+
         def first(r, carry):
             out, values = stencil(odd, r)
             at = pl.ds(r, ROW_STEP)
@@ -666,21 +709,21 @@
                 basis[0, p, at, :] = v
                 if carry is not None:
                     square, total = carry
-                    carry = (add_to(square, p, fold(v * v)), add_to(total, p, fold(v * ocean[p, at, :])))
+                    carry = (
+                        add_to(square, p, fold(v * v)),
+                        add_to(total, p, fold(v)) if with_totals else total,
+                    )
             return carry
 
         (square,) = over_bands(first, 0, (zero_pair,))
         sums[64:65, :] = jnp.sum(own_total(square), axis=0, keepdims=True)
 
-        def step(j, source, target):
-            new_part = jnp.where(j == 1, 0.5, 1.0)
-            old_part = jnp.where(j == 1, 0.0, 1.0)
-
+        def step(j, source, target, is_first=False):
             def chunk(r, carry):
                 out, values = stencil(source, r)
                 at = pl.ds(r, ROW_STEP)
                 for p in range(panels):
-                    v = new_part * out[p] - old_part * target[p, at, :]
+                    v = 0.5 * out[p] if is_first else out[p] - target[p, at, :]
                     target[p, at, :] = v
                     basis[j, p, at, :] = v
                     if carry is not None:
@@ -688,20 +731,22 @@
                         carry = (
                             add_to(square, p, fold(v * v)),
                             add_to(cross, p, fold(v * values[p])),
-                            add_to(total, p, fold(v * ocean[p, at, :])),
+                            add_to(total, p, fold(v)) if with_totals else total,
                         )
                 return carry
 
             square, cross = over_bands(chunk, j * bands, (zero_pair, zero_pair))
-            sums[pl.ds(64 + j, 1), :] = jnp.sum(own_total(square), axis=0, keepdims=True)
-            sums[pl.ds(80 + j, 1), :] = jnp.sum(own_total(cross), axis=0, keepdims=True)
+            sums[row_at(64 + j), :] = jnp.sum(own_total(square), axis=0, keepdims=True)
+            sums[row_at(80 + j), :] = jnp.sum(own_total(cross), axis=0, keepdims=True)
 
         def two_steps(i, carry):
-            step(2 * i + 1, even, odd)
             step(2 * i + 2, odd, even)
+            step(2 * i + 3, even, odd)
             return carry
 
-        lax.fori_loop(0, KB // 2, two_steps, 0)
+        step(1, even, odd, True)
+        lax.fori_loop(0, KB // 2 - 1, two_steps, 0)
+        step(KB, odd, even)
 
         row = lax.dot_general(
             jnp.ones((8, LANES), jnp.float32),
@@ -710,21 +755,16 @@
             precision=highest,
             preferred_element_type=jnp.float32,
         )
-        (start_gx, wait_gx, _), (start_gy, wait_gy, _) = gram_phases[cycle]
-        gram_x[cycle, gx] = jnp.where(sub == gx, row, 0.0)
-        start_gx()
+        start_g, wait_g, _ = grams[cycle]
+        start_g(row[0:1])
         if cycle == 0:
             choose_rows()
+            wait_by()
+            permute_rows()
         else:
             lax.fori_loop(0, LANES // 16, choose_back, 0)
-        wait_gx()
-        gram_y[cycle, gy] = total_of(gram_x.at[cycle], size_x)
-        start_gy()
-        if cycle == 0:
-            wait_by()
-            permute_rows()
-        wait_gy()
-        gathered = [gram_y[cycle, i] for i in range(size_y)]
+        wait_g()
+        gathered = [gram_all[cycle, 8 * i : 8 * i + 8, :] for i in range(groups)]
         whole = sub_total(functools.reduce(jnp.add, gathered))
 
         def at_lane(k):
@@ -743,19 +783,18 @@
             mix = jnp.where(group == 0, 1.0, 0.0)
             for a in range(KB + 1):
                 mix = jnp.where(group == a, mix - combined[a], mix)
-            rhs = zero8
-            for i in range(size_y):
-                part = gathered[i] * jnp.where(lane8 < (KB + 1) * bands, mix, 0.0)
+            mix = jnp.where(lane8 < (KB + 1) * bands, mix, 0.0)
+            mixed = []
+            for part in gathered:
+                part = part * mix
                 move = bands
                 while move < LANES:
                     part = part + pltpu.roll(part, move, 1)
                     move *= 2
-                rhs = jnp.where(group == i, part, rhs)
-            found = permuted[0] * rhs[0:1, :]
-            for i in range(1, size_x):
-                found = found + permuted[i] * rhs[i : i + 1, :]
-            found = jnp.broadcast_to(jnp.sum(found, axis=1, keepdims=True), found.shape)
-            next_values = [jnp.broadcast_to(found[k : k + 1, :], (8, LANES)) for k in range(3 * len(strips))]
+                mixed.append(part)
+            found = chosen[...] * by_label(mixed)
+            found = jnp.broadcast_to(jnp.sum(found, axis=1, keepdims=True), (found.shape[0], LANES))
+            next_values = [jnp.broadcast_to(found[k : k + 1, :], (8, LANES)) for k in range(len(labels))]
 
         w = [tall(factors[j], ROW_STEP) for j in range(KB)]
         c_all = [tall(factors[KB + a], ROW_STEP) for a in range(KB + 1)]
@@ -822,6 +861,7 @@
     any_spec = pl.BlockSpec(memory_space=pltpu.MemorySpace.HBM)
     vmem = pl.BlockSpec(memory_space=pltpu.VMEM)
     smem = pl.BlockSpec(memory_space=pltpu.SMEM)
+    rows_all = pltpu.VMEM((size_x * size_y, LANES), f32)
     tiles = lambda *lead: pltpu.VMEM(lead + (8, LANES), f32)
     dma = pltpu.SemaphoreType.DMA
     n_agg = coarse_inverse.shape[1]
@@ -861,26 +901,22 @@
             pltpu.VMEM((4, DEPTH, LANES), f32),
             pltpu.VMEM((4, DEPTH, LANES), f32),
             pltpu.VMEM((2, 2, DEPTH, breadth), f32),
-            tiles(bands),
+            pltpu.VMEM((8, -(-n_agg // LANES) * LANES), f32),
             pltpu.VMEM((wanted, n_agg), f32),
-            pltpu.VMEM((size_x, wanted, LANES), f32),
+            pltpu.VMEM((wanted, -(-n_agg // LANES) * LANES), f32),
             pltpu.VMEM((size_x, bands, n_agg), f32),
             pltpu.VMEM((size_y, size_x * bands, n_agg), f32),
             pltpu.VMEM((LANES, LANES), f32),
             tiles(2 * KB + 1),
-            tiles(size_x, 2),
-            tiles(size_y, 2),
-            tiles(size_x),
-            tiles(size_y),
-            tiles(size_x),
-            tiles(size_y),
-            tiles(CYCLES, size_x),
-            tiles(CYCLES, size_y),
+            rows_all,
+            rows_all,
+            rows_all,
+            pltpu.VMEM((CYCLES, size_x * size_y, LANES), f32),
             dma((4,)),
             dma((10,)),
             dma((10,)),
-            dma((14,)),
-            dma((14,)),
+            dma((7,)),
+            dma((7,)),
         ],
         compiler_params=pltpu.CompilerParams(
             collective_id=0, has_side_effects=True, vmem_limit_bytes=40 * 1024 * 1024

time: 66.4 us -> 62.2 us (0.937)
  Pallas kernels: 65.6 us -> 61.4 us
    pallas_call x1, Pallas kernels: 62.9 us -> 58.7 us  [on_device(): pl.pallas_call(functools.partial(kernel, size_x, size_y), out_shape=(deal...]
where the time goes in v4:
time: 62.2 us; the launch traced here: 62 us
  Pallas kernels  61.4 us (99%)
  between operations  0.64 us (1%)
    pallas_call x1, Pallas kernels, on_device(): pl.pallas_call(functools.partial(kernel, size_x, size_y), out_shape=(deal...  58.7 us
    pallas_call x1, Pallas kernels, on_device(): pl.pallas_call(to_natural, out_shape=(jax.ShapeDtypeStruct((height, bread...  2.7 us

profile of v4, /device:TPU:1, one launch (start us, length us, event | category | flops | bytes accessed | tf_op | source)
XLA Modules:
  0.0 62.0 jit_solution(10429904926917312648)
XLA Ops:
  0.6 58.7 %shard_map.68 = (f32[5,256,128]{2,1,0:T(8,128)S(1)}, f32[5,256,128]{2,1,0:T(8,128)S(1)}, bf16[640,512]{1,0:T(8,128)(2,1)S(1)}) custom-call(f32[256,512]{1,0:T(8,128)} %forcing_ref.1, f32[256,512]{1,0:T(8,128)} %depth_ref.1, s32[256,512]{1,0:T(8,128)} %mask_ref.1, s32[4,8]{1,0:T(4,128)} %agg_ref.1, f32[4,512]{1,0:T(4,128)} %inverse_ref.1), custom_call_target="tpu_custom_call" | custom-call | tf_op jit(solution)/shard_map/pallas_call | solution.py:875
  59.3 2.7 %shard_map.69 = (f32[256,512]{1,0:T(8,128)}, f32[256,512]{1,0:T(8,128)}) custom-call(f32[5,256,128]{2,1,0:T(8,128)S(1)} %get-tuple-element.5.solution_ref, f32[5,256,128]{2,1,0:T(8,128)S(1)} %get-tuple-element.6.residual_ref, bf16[640,512]{1,0:T(8,128)(2,1)S(1)} %get-tuple-element.7.back), custom_call_target="tpu_custom_call" | custom-call | tf_op jit(solution)/shard_map/pallas_call | solution.py:927

commit v5 on v4

--- a/solution.py
+++ b/solution.py
@@ -51,10 +51,9 @@
 
 
 def placed(x, chooser):
-    high, low = split(x)
-    return jnp.dot(high, chooser, preferred_element_type=jnp.float32) + jnp.dot(
-        low, chooser, preferred_element_type=jnp.float32
-    )
+    rows = x.shape[0]
+    both = jnp.dot(jnp.concatenate(split(x), axis=0), chooser, preferred_element_type=jnp.float32)
+    return both[0:rows] + both[rows:]
 
 
 def exact_placed(chooser, x):
@@ -145,15 +144,16 @@
     mask_ref,
     agg_ref,
     inverse_ref,
-    solution_ref,
-    residual_ref,
-    back,
+    natural,
+    natural_sol,
+    factors,
     in_f,
     in_b,
     in_m,
     side_w,
     side_r,
     chooser,
+    back,
     wet,
     ocean,
     res,
@@ -177,7 +177,6 @@
     bulk_x,
     bulk_y,
     sums,
-    factors,
     first_all,
     max_all,
     coarse_all,
@@ -418,6 +417,18 @@
         label = (agg_ref[t, 0] + 1).astype(jnp.float32)
         first_row_values = jnp.where(lane8 == bands + t, label, first_row_values)
 
+    def choose_back(c, carry):
+        for p in range(panels):
+            for q in range(own_panels):
+                goal, lane = place(16, LANES, q * LANES, True)
+                rows = pl.ds(p * LANES + c * 16, 16)
+                back[rows, q * LANES : (q + 1) * LANES] = jnp.where(
+                    goal == (lane + c * 16) * panels + p, 1.0, 0.0
+                ).astype(jnp.bfloat16)
+        return carry
+
+    lax.fori_loop(0, LANES // 16, choose_back, 0)
+
     pl.semaphore_wait(barrier, others)
     for copy in halos:
         copy.start()
@@ -432,7 +443,7 @@
     start_bx()
 
     own_rows = pl.ds(0, breadth)
-    block_rows = 64
+    block_rows = min(256, height)
 
     def settle(c, carry):
         rows = pl.ds(c * block_rows, block_rows)
@@ -655,14 +666,18 @@
             rows = part if rows is None else rows + part
         chosen[:, 0:n_agg] = rows
 
-    def choose_back(c, carry):
-        for p in range(panels):
-            for q in range(own_panels):
-                goal, lane = place(16, LANES, q * LANES, True)
-                rows = pl.ds(p * LANES + c * 16, 16)
-                back[rows, q * LANES : (q + 1) * LANES] = jnp.where(
-                    goal == (lane + c * 16) * panels + p, 1.0, 0.0
-                ).astype(jnp.bfloat16)
+    blocks = height // block_rows
+
+    def basis_to_natural(i, carry):
+        a, c = lax.div(i, blocks), lax.rem(i, blocks)
+        at = pl.ds(pl.multiple_of(OWN + c * block_rows, 8), block_rows)
+        rows = pl.ds(pl.multiple_of(c * block_rows, 8), block_rows)
+        natural[a, rows, :] = placed(jnp.concatenate([basis[a, p, at, :] for p in range(panels)], axis=1), back[...])
+        return carry
+
+    def sol_to_natural(c, carry):
+        rows = pl.ds(c * block_rows, block_rows)
+        natural_sol[rows, :] = placed(jnp.concatenate([sol[p, rows, :] for p in range(panels)], axis=1), back[...])
         return carry
 
     next_values = None
@@ -762,7 +777,8 @@
             wait_by()
             permute_rows()
         else:
-            lax.fori_loop(0, LANES // 16, choose_back, 0)
+            lax.fori_loop(0, (KB + 1) * blocks, basis_to_natural, 0)
+            lax.fori_loop(0, blocks, sol_to_natural, 0)
         wait_g()
         gathered = [gram_all[cycle, 8 * i : 8 * i + 8, :] for i in range(groups)]
         whole = sub_total(functools.reduce(jnp.add, gathered))
@@ -796,6 +812,8 @@
             found = jnp.broadcast_to(jnp.sum(found, axis=1, keepdims=True), (found.shape[0], LANES))
             next_values = [jnp.broadcast_to(found[k : k + 1, :], (8, LANES)) for k in range(len(labels))]
 
+        if cycle == CYCLES - 1:
+            break
         w = [tall(factors[j], ROW_STEP) for j in range(KB)]
         c_all = [tall(factors[KB + a], ROW_STEP) for a in range(KB + 1)]
 
@@ -812,12 +830,8 @@
             answer = sol[p, rows, :]
             for j in range(KB):
                 answer = answer + w[j] * values[j]
-            if cycle < CYCLES - 1:
-                res[p, at, :] = residual
-                sol[p, rows, :] = answer
-            else:
-                residual_ref[p, rows, :] = residual
-                solution_ref[p, rows, :] = answer
+            res[p, at, :] = residual
+            sol[p, rows, :] = answer
 
         def update_own(c, carry):
             for p in range(panels):
@@ -825,26 +839,41 @@
             return carry
 
         lax.fori_loop(0, height // ROW_STEP, update_own, 0)
-        if cycle < CYCLES - 1:
-            for p in range(panels):
-                update(PAD, p, None)
-                update(OWN + height, p, None)
+        for p in range(panels):
+            update(PAD, p, None)
+            update(OWN + height, p, None)
 
     for done in finish:
         done()
 
 
-def to_natural(solution_ref, residual_ref, back, solution_out, residual_out, parts, sems):
-    panels, height = solution_ref.shape[:2]
+def combine(natural, natural_sol, factors, solution_out, residual_out, parts, sems):
+    height, breadth = natural_sol.shape
     rows = parts.shape[1]
     copies = []
     for index in range(height // rows):
-        at = pl.ds(index * rows, rows)
-        for which, (source, target) in enumerate(((solution_ref, solution_out), (residual_ref, residual_out))):
+
+        def chunk(c, carry, index=index):
+            at = pl.ds(index * rows + c * ROW_STEP, ROW_STEP)
+            there = pl.ds(c * ROW_STEP, ROW_STEP)
+            for p in range(breadth // LANES):
+                columns = slice(p * LANES, (p + 1) * LANES)
+                values = [natural[a, at, columns] for a in range(KB + 1)]
+                answer, residual = natural_sol[at, columns], values[0]
+                for a in range(KB + 1):
+                    residual = residual - tall(factors[KB + a], ROW_STEP) * values[a]
+                for j in range(KB):
+                    answer = answer + tall(factors[j], ROW_STEP) * values[j]
+                parts[2 * index, there, columns] = answer
+                parts[2 * index + 1, there, columns] = residual
+            return carry
+
+        lax.fori_loop(0, rows // ROW_STEP, chunk, 0)
+        for which, target in enumerate((solution_out, residual_out)):
             slot = 2 * index + which
-            parts[slot] = placed(jnp.concatenate([source[p, at, :] for p in range(panels)], axis=1), back[...])
-            copies.append(pltpu.make_async_copy(parts.at[slot], target.at[at, :], sems.at[slot]))
-            copies[-1].start()
+            copy = pltpu.make_async_copy(parts.at[slot], target.at[pl.ds(index * rows, rows), :], sems.at[slot])
+            copy.start()
+            copies.append(copy)
     for copy in copies:
         copy.wait()
 
@@ -866,15 +895,18 @@
     dma = pltpu.SemaphoreType.DMA
     n_agg = coarse_inverse.shape[1]
     wanted = -(-3 * (bands + 2) // 8) * 8
-    dealt = jax.ShapeDtypeStruct((panels, height, LANES), f32)
-    back = jax.ShapeDtypeStruct((panels * LANES, breadth), jnp.bfloat16)
+    results = (
+        jax.ShapeDtypeStruct((KB + 1, height, breadth), f32),
+        jax.ShapeDtypeStruct((height, breadth), f32),
+        jax.ShapeDtypeStruct((2 * KB + 1, 8, LANES), f32),
+    )
     forcing, bathymetry, ocean_mask, aggregate_id, coarse_inverse = (
         pltpu.with_memory_space_constraint(x, pltpu.MemorySpace.HBM)
         for x in (forcing, bathymetry, ocean_mask, aggregate_id, coarse_inverse)
     )
-    answer, residual, back = pl.pallas_call(
+    natural, natural_sol, factors = pl.pallas_call(
         functools.partial(kernel, size_x, size_y),
-        out_shape=(dealt, dealt, back),
+        out_shape=results,
         in_specs=[any_spec, any_spec, any_spec, smem, any_spec],
         out_specs=(vmem, vmem, vmem),
         scratch_shapes=[
@@ -884,6 +916,7 @@
             pltpu.VMEM((height, LANES), f32),
             pltpu.VMEM((height, LANES), f32),
             pltpu.VMEM((panels * LANES, panels * LANES), jnp.bfloat16),
+            pltpu.VMEM((panels * LANES, breadth), jnp.bfloat16),
             field,
             field,
             field,
@@ -907,7 +940,6 @@
             pltpu.VMEM((size_x, bands, n_agg), f32),
             pltpu.VMEM((size_y, size_x * bands, n_agg), f32),
             pltpu.VMEM((LANES, LANES), f32),
-            tiles(2 * KB + 1),
             rows_all,
             rows_all,
             rows_all,
@@ -925,13 +957,13 @@
     part = 64
     count = 2 * (height // part)
     return pl.pallas_call(
-        to_natural,
+        combine,
         out_shape=(jax.ShapeDtypeStruct((height, breadth), f32),) * 2,
         in_specs=[vmem, vmem, vmem],
         out_specs=(any_spec, any_spec),
         scratch_shapes=[pltpu.VMEM((count, part, breadth), f32), dma((count,))],
         compiler_params=pltpu.CompilerParams(vmem_limit_bytes=16 * 1024 * 1024),
-    )(answer, residual, back)
+    )(natural, natural_sol, factors)
 
 
 def solution(mesh):

time: 62.2 us -> 59.3 us (0.953)
  Pallas kernels: 61.4 us -> 58.5 us
    pallas_call x2, Pallas kernels: 61.4 us -> 58.5 us  [the longest x1 57 us: on_device(): pl.pallas_call(functools.partial(kernel, size_x, size_y), out_shape=resul...]
where the time goes in v5:
time: 59.3 us; the launch traced here: 59.2 us
  Pallas kernels  58.5 us (99%)
  between operations  0.64 us (1%)
    pallas_call x1, Pallas kernels, on_device(): pl.pallas_call(functools.partial(kernel, size_x, size_y), out_shape=resul...  57 us
    pallas_call x1, Pallas kernels, on_device(): pl.pallas_call(combine, out_shape=(jax.ShapeDtypeStruct((height, breadth)...  1.52 us

profile of v5, /device:TPU:1, one launch (start us, length us, event | category | flops | bytes accessed | tf_op | source)
XLA Modules:
  0.0 59.2 jit_solution(17653297825002304191)
XLA Ops:
  0.6 57.0 %shard_map.68 = (f32[9,256,512]{2,1,0:T(8,128)S(1)}, f32[256,512]{1,0:T(8,128)S(1)}, f32[17,8,128]{2,1,0:T(8,128)S(1)}) custom-call(f32[256,512]{1,0:T(8,128)} %forcing_ref.1, f32[256,512]{1,0:T(8,128)} %depth_ref.1, s32[256,512]{1,0:T(8,128)} %mask_ref.1, s32[4,8]{1,0:T(4,128)} %agg_ref.1, f32[4,512]{1,0:T(4,128)} %inverse_ref.1), custom_call_target="tpu_custom_call" | custom-call | tf_op jit(solution)/shard_map/pallas_call | solution.py:907
  57.6 1.5 %shard_map.69 = (f32[256,512]{1,0:T(8,128)}, f32[256,512]{1,0:T(8,128)}) custom-call(f32[9,256,512]{2,1,0:T(8,128)S(1)} %get-tuple-element.5.natural, f32[256,512]{1,0:T(8,128)S(1)} %get-tuple-element.6.natural_sol, f32[17,8,128]{2,1,0:T(8,128)S(1)} %get-tuple-element.7.factors), custom_call_target="tpu_custom_call" | custom-call | tf_op jit(solution)/shard_map/pallas_call | solution.py:959

commit v6 on v5

--- a/solution.py
+++ b/solution.py
@@ -598,7 +598,7 @@
         return carry
 
     chunks_all = (rows_all - 2 * PAD) // ROW_STEP
-    lax.fori_loop(0, chunks_all, rescale, 0)
+    lax.fori_loop(0, chunks_all, rescale, 0, unroll=3)
 
     def stencil(array, r):
         at = pl.ds(r, ROW_STEP)
@@ -704,7 +704,7 @@
                         sol[p, inner, :] = value if cycle == 0 else sol[p, inner, :] + value
                 return carry
 
-            lax.fori_loop(0, chunks, body, 0)
+            lax.fori_loop(0, chunks, body, 0, unroll=True)
 
         spread_band(0, PAD, DEPTH // ROW_STEP)
         for t in range(bands):
@@ -838,7 +838,7 @@
                 update(OWN + c * ROW_STEP, p, c * ROW_STEP)
             return carry
 
-        lax.fori_loop(0, height // ROW_STEP, update_own, 0)
+        lax.fori_loop(0, height // ROW_STEP, update_own, 0, unroll=2)
         for p in range(panels):
             update(PAD, p, None)
             update(OWN + height, p, None)
@@ -868,7 +868,7 @@
                 parts[2 * index + 1, there, columns] = residual
             return carry
 
-        lax.fori_loop(0, rows // ROW_STEP, chunk, 0)
+        lax.fori_loop(0, rows // ROW_STEP, chunk, 0, unroll=2)
         for which, target in enumerate((solution_out, residual_out)):
             slot = 2 * index + which
             copy = pltpu.make_async_copy(parts.at[slot], target.at[pl.ds(index * rows, rows), :], sems.at[slot])

time: 59.3 us -> 59 us (level)
  no operation moved by 1% of the time
where the time goes in v6:
time: 59 us; the launch traced here: 58.9 us
  Pallas kernels  58.3 us (99%)
  between operations  0.64 us (1%)
    pallas_call x1, Pallas kernels, on_device(): pl.pallas_call(functools.partial(kernel, size_x, size_y), out_shape=resul...  56.8 us
    pallas_call x1, Pallas kernels, on_device(): pl.pallas_call(combine, out_shape=(jax.ShapeDtypeStruct((height, breadth)...  1.48 us

profile of v6, /device:TPU:1, one launch (start us, length us, event | category | flops | bytes accessed | tf_op | source)
XLA Modules:
  0.0 58.9 jit_solution(11504798024429730587)
XLA Ops:
  0.6 56.8 %shard_map.68 = (f32[9,256,512]{2,1,0:T(8,128)S(1)}, f32[256,512]{1,0:T(8,128)S(1)}, f32[17,8,128]{2,1,0:T(8,128)S(1)}) custom-call(f32[256,512]{1,0:T(8,128)} %forcing_ref.1, f32[256,512]{1,0:T(8,128)} %depth_ref.1, s32[256,512]{1,0:T(8,128)} %mask_ref.1, s32[4,8]{1,0:T(4,128)} %agg_ref.1, f32[4,512]{1,0:T(4,128)} %inverse_ref.1), custom_call_target="tpu_custom_call" | custom-call | tf_op jit(solution)/shard_map/pallas_call | solution.py:907
  57.4 1.5 %shard_map.69 = (f32[256,512]{1,0:T(8,128)}, f32[256,512]{1,0:T(8,128)}) custom-call(f32[9,256,512]{2,1,0:T(8,128)S(1)} %get-tuple-element.5.natural, f32[256,512]{1,0:T(8,128)S(1)} %get-tuple-element.6.natural_sol, f32[17,8,128]{2,1,0:T(8,128)S(1)} %get-tuple-element.7.factors), custom_call_target="tpu_custom_call" | custom-call | tf_op jit(solution)/shard_map/pallas_call | solution.py:959
